TPU v7x, 32 devices: a whole 2x2x4 slice. The times are simulated.
32 devices in a mesh: dp: 4 (over z), context: 2 (over core), tensor: 4 (over y, x).
Axes of the slice: x: 2, y: 2, z: 4, core: 2. Of those that a mesh axis runs over, the one named last changes fastest.
Arguments:
- tokens: bfloat16 [12, 2048, 768], P('dp', ('context', 'tensor')), may hold values from -6 to 6
- segments: int32 [12, 2048], P('dp'), may hold values from 0 to 7, never falling along the last dimension, each value on 1 to 1792 neighbouring positions
- w_qkv: bfloat16 [768, 3, 768], P('dp', None, 'tensor'), may hold values from -0.21875 to 0.21875
- w_out: bfloat16 [768, 768], P('tensor', 'dp'), may hold values from -1.5 to 1.5
- w_in: bfloat16 [768, 3072], P('dp', 'tensor'), may hold values from -0.21875 to 0.21875
- w_back: bfloat16 [3072, 768], P('tensor', 'dp'), may hold values from -0.109375 to 0.109375
- gain_attn: bfloat16 [768], P('dp'), may hold values from 0.25 to 1.75
- gain_mlp: bfloat16 [768], P('dp'), may hold values from 0.25 to 1.75
- cotangent: bfloat16 [12, 2048, 768], P('dp', ('context', 'tensor')), may hold values from -6 to 6
Outputs:
- output: bfloat16 [12, 2048, 768], P('dp', ('context', 'tensor'))
- grad_tokens: bfloat16 [12, 2048, 768], P('dp', ('context', 'tensor'))
- grad_w_qkv: float32 [768, 3, 768], P('dp', None, 'tensor')
- grad_w_out: float32 [768, 768], P('tensor', 'dp')
- grad_w_in: float32 [768, 3072], P('dp', 'tensor')
- grad_w_back: float32 [3072, 768], P('tensor', 'dp')
- grad_gain_attn: float32 [768], P('dp')
- grad_gain_mlp: float32 [768], P('dp')
Inputs may be any that keep to these rules, and one draw needn't show every extreme that they name: `segments`: within a sequence the numbers never fall; a document holds 1 to 1792 bytes, and some document holds exactly 1792.
All inputs are finite; a program needn't handle non-finite values.
Results may differ from a plain program's by a relative error of at most 0.02.
Values may be sent and summed in bfloat16 or wider, within the bound.
A program may use at most 192 MiB of HBM per device.

v0:
```python
import math

import jax
import jax.numpy as jnp
from jax import lax
from jax.sharding import PartitionSpec as P

HD = 64
WIN = 1536
QB = 512


epsilon = 1e-06


def passed_along(array, axis, by):
    length = lax.axis_size(axis)
    pairs = [(i, i + by) for i in range(length) if 0 <= i + by < length]
    return lax.ppermute(array, axis, pairs)


def rms_local(values, gain):
    return values * lax.rsqrt(jnp.mean(values * values, axis=-1, keepdims=True) + epsilon) * gain


def gelu_tanh(values):
    return jax.nn.gelu(values, approximate=True)


def contract_rows(left, right):
    return lax.dot_general(
        left, right, (((0,), (0,)), ((), ())), preferred_element_type=jnp.float32
    )


def inner_t(left, right):
    return lax.dot_general(
        left, right, (((1,), (1,)), ((), ())), preferred_element_type=jnp.float32
    )


def window_mask(query_pos, key_pos, query_seg, key_seg):
    return (
        (key_pos[None, :] >= 0)
        & (key_pos[None, :] <= query_pos[:, None])
        & (query_pos[:, None] - key_pos[None, :] < WIN)
        & (query_seg[:, None] == key_seg[None, :])
    )


def per_device(tokens, segments, w_qkv, w_out, w_in, w_back, gain_attn, gain_mlp, cotangent):
    gathered = (
        lax.all_gather(w_qkv, "dp", axis=0, tiled=True),
        lax.all_gather(w_out, "dp", axis=1, tiled=True),
        lax.all_gather(w_in, "dp", axis=0, tiled=True),
        lax.all_gather(w_back, "dp", axis=1, tiled=True),
        lax.all_gather(gain_attn, "dp", axis=0, tiled=True),
        lax.all_gather(gain_mlp, "dp", axis=0, tiled=True),
    )
    w_attn, w_proj, w_up, w_down, gain_one, gain_two = gathered
    sequences, own_rows, model_width = tokens.shape
    tensor_count = lax.axis_size("tensor")
    span_rows = own_rows * tensor_count
    local_width = w_qkv.shape[2]
    local_heads = local_width // HD
    total_len = segments.shape[1]
    context_rank = lax.axis_index("context")
    block_count = span_rows // QB
    key_span = min(2 * span_rows, WIN + QB)
    score_scale = 1.0 / math.sqrt(HD)

    def gather_rows(values):
        return lax.all_gather(values, "tensor", axis=1, tiled=True)

    def scatter_rows(values):
        return lax.psum_scatter(
            values.astype(jnp.bfloat16), "tensor", scatter_dimension=1, tiled=True
        ).astype(jnp.float32)

    def branch_reduce(values):
        return lax.psum_scatter(
            values.astype(jnp.bfloat16), "tensor", scatter_dimension=1, tiled=True
        ).astype(jnp.float32)

    inputs = tokens.astype(jnp.float32)
    gain_first = gain_one.astype(jnp.float32)
    gain_second = gain_two.astype(jnp.float32)
    normed_one = rms_local(inputs, gain_first).astype(jnp.bfloat16)
    flat_one = gather_rows(normed_one).reshape(sequences * span_rows, model_width)
    projected = jnp.dot(
        flat_one, w_attn.reshape(model_width, 3 * local_width), preferred_element_type=jnp.float32
    )
    projected = projected.astype(jnp.bfloat16).reshape(sequences, span_rows, 3, local_width)
    earlier = passed_along(projected[:, :, 1:], "context", 1)
    keyval = jnp.concatenate([earlier, projected[:, :, 1:]], axis=1).reshape(
        sequences, 2 * span_rows, 2, local_heads, HD
    )
    queries = projected[:, :, 0].reshape(sequences, span_rows, local_heads, HD)

    def block_setup(flat_index):
        sequence = flat_index // block_count
        query_start = flat_index % block_count * QB
        key_start = jnp.clip(span_rows + query_start + QB - key_span, 0, 2 * span_rows - key_span)
        query_block = lax.dynamic_slice_in_dim(
            lax.dynamic_index_in_dim(queries, sequence, 0, False), query_start, QB, 0
        )
        keyval_block = lax.dynamic_index_in_dim(keyval, sequence, 0, False)
        segrow = lax.dynamic_index_in_dim(segments, sequence, 0, False)
        query_pos = context_rank * span_rows + query_start + jnp.arange(QB, dtype=jnp.int32)
        key_pos = (context_rank - 1) * span_rows + key_start + jnp.arange(key_span, dtype=jnp.int32)
        query_seg = jnp.take(segrow, query_pos)
        key_seg = jnp.take(segrow, jnp.clip(key_pos, 0, total_len - 1))
        allowed = window_mask(query_pos, key_pos, query_seg, key_seg)
        scores = (
            jnp.einsum(
                "qhd,khd->hqk", query_block, keyval_block[:, 0], preferred_element_type=jnp.float32
            )
            * score_scale
        )
        scores = jnp.where(allowed[None], scores, -1e30)
        return (sequence, query_start, key_start, query_block, keyval_block, allowed, scores)

    def forward_block(flat_index):
        _, _, _, _, keyval_block, _, scores = block_setup(flat_index)
        row_max = jnp.max(scores, axis=-1, keepdims=True)
        exponent = jnp.exp(scores - row_max)
        denominator = jnp.sum(exponent, axis=-1, keepdims=True)
        soft_low = (exponent / denominator).astype(jnp.bfloat16)
        attended_block = jnp.einsum(
            "hqk,khd->qhd", soft_low, keyval_block[:, 1], preferred_element_type=jnp.float32
        )
        return (attended_block.astype(jnp.bfloat16), (row_max + jnp.log(denominator))[..., 0])

    attended_blocks, log_totals = lax.map(
        forward_block, jnp.arange(sequences * block_count, dtype=jnp.int32)
    )
    attended = attended_blocks.reshape(sequences * span_rows, local_width)
    attention_out = branch_reduce(
        jnp.dot(attended, w_proj, preferred_element_type=jnp.float32).reshape(
            sequences, span_rows, model_width
        )
    )
    middle = inputs + attention_out
    normed_two = rms_local(middle, gain_second).astype(jnp.bfloat16)
    rows_two = gather_rows(normed_two).reshape(sequences * span_rows, model_width)
    hidden_pre = jnp.dot(rows_two, w_up, preferred_element_type=jnp.float32)
    activated = gelu_tanh(hidden_pre).astype(jnp.bfloat16)
    branch = branch_reduce(
        jnp.dot(activated, w_down, preferred_element_type=jnp.float32).reshape(
            sequences, span_rows, model_width
        )
    )
    result = (middle + branch).astype(jnp.bfloat16)
    grad_rows = gather_rows(cotangent).reshape(sequences * span_rows, model_width)
    grad_down = contract_rows(activated, grad_rows)
    grad_active = inner_t(grad_rows, w_down)
    _, gelu_pull = jax.vjp(gelu_tanh, hidden_pre)
    grad_hidden = gelu_pull(grad_active)[0].astype(jnp.bfloat16)
    grad_up = contract_rows(rows_two, grad_hidden)
    grad_norm_two = scatter_rows(
        inner_t(grad_hidden, w_up).reshape(sequences, span_rows, model_width)
    )
    _, pull_two = jax.vjp(rms_local, middle, gain_second)
    grad_middle_norm, grad_gain_two = pull_two(grad_norm_two)
    grad_middle = cotangent.astype(jnp.float32) + grad_middle_norm
    grad_attn_rows = gather_rows(grad_middle.astype(jnp.bfloat16)).reshape(
        sequences * span_rows, model_width
    )
    grad_proj = contract_rows(attended, grad_attn_rows)
    grad_attended = (
        inner_t(grad_attn_rows, w_proj)
        .astype(jnp.bfloat16)
        .reshape(sequences, span_rows, local_heads, HD)
    )

    def backward_sequence(sequence_index):

        def backward_step(totals, block_index):
            flat_index = sequence_index * block_count + block_index
            sequence, query_start, key_start, query_block, keyval_block, allowed, scores = (
                block_setup(flat_index)
            )
            log_total = lax.dynamic_index_in_dim(log_totals, flat_index, 0, False)
            soft = jnp.where(allowed[None], jnp.exp(scores - log_total[..., None]), 0.0)
            grad_out = lax.dynamic_slice_in_dim(
                lax.dynamic_index_in_dim(grad_attended, sequence, 0, False), query_start, QB, 0
            )
            grad_prob = jnp.einsum(
                "qhd,khd->hqk", grad_out, keyval_block[:, 1], preferred_element_type=jnp.float32
            )
            row_delta = jnp.sum(soft * grad_prob, axis=-1, keepdims=True)
            grad_score = (soft * (grad_prob - row_delta)).astype(jnp.bfloat16)
            grad_query = (
                jnp.einsum(
                    "hqk,khd->qhd",
                    grad_score,
                    keyval_block[:, 0],
                    preferred_element_type=jnp.float32,
                )
                * score_scale
            ).astype(jnp.bfloat16)
            grad_key = (
                jnp.einsum(
                    "hqk,qhd->khd", grad_score, query_block, preferred_element_type=jnp.float32
                )
                * score_scale
            )
            grad_value = jnp.einsum(
                "hqk,qhd->khd",
                soft.astype(jnp.bfloat16),
                grad_out,
                preferred_element_type=jnp.float32,
            )
            update = jnp.stack([grad_key, grad_value], axis=1)
            current = totals
            totals = current + update
            return (totals, grad_query)

        zeros_init = jnp.zeros((2 * span_rows, 2, local_heads, HD), jnp.float32)
        totals, grad_queries = lax.scan(
            backward_step, zeros_init, jnp.arange(block_count, dtype=jnp.int32)
        )
        return (grad_queries.reshape(span_rows, local_heads, HD), totals)

    grad_queries, grad_keyval = lax.map(backward_sequence, jnp.arange(sequences, dtype=jnp.int32))
    returned = passed_along(grad_keyval[:, :span_rows].astype(jnp.bfloat16), "context", -1).astype(
        jnp.float32
    )
    own_keyval = (
        (grad_keyval[:, span_rows:] + returned)
        .astype(jnp.bfloat16)
        .reshape(sequences, span_rows, 2, local_width)
    )
    grad_projected = jnp.concatenate(
        [grad_queries.reshape(sequences, span_rows, 1, local_width), own_keyval], axis=2
    )
    grad_projected = grad_projected.reshape(sequences * span_rows, 3 * local_width)
    grad_attn_w = contract_rows(flat_one, grad_projected).reshape(model_width, 3, local_width)
    grad_norm_one = scatter_rows(
        inner_t(grad_projected, w_attn.reshape(model_width, 3 * local_width)).reshape(
            sequences, span_rows, model_width
        )
    )
    _, pull_one = jax.vjp(rms_local, inputs, gain_first)
    grad_input_norm, grad_gain_one = pull_one(grad_norm_one)
    grad_input = (grad_middle + grad_input_norm).astype(jnp.bfloat16)
    gain_totals = lax.psum((grad_gain_one, grad_gain_two), "tensor")
    shards = (
        lax.psum_scatter(
            grad_attn_w.astype(jnp.bfloat16), "dp", scatter_dimension=0, tiled=True
        ).astype(jnp.float32),
        lax.psum_scatter(
            grad_proj.astype(jnp.bfloat16), "dp", scatter_dimension=1, tiled=True
        ).astype(jnp.float32),
        lax.psum_scatter(
            grad_up.astype(jnp.bfloat16), "dp", scatter_dimension=0, tiled=True
        ).astype(jnp.float32),
        lax.psum_scatter(
            grad_down.astype(jnp.bfloat16), "dp", scatter_dimension=1, tiled=True
        ).astype(jnp.float32),
        lax.psum_scatter(
            gain_totals[0].astype(jnp.bfloat16), "dp", scatter_dimension=0, tiled=True
        ).astype(jnp.float32),
        lax.psum_scatter(
            gain_totals[1].astype(jnp.bfloat16), "dp", scatter_dimension=0, tiled=True
        ).astype(jnp.float32),
    )
    owned = (
        lax.psum(shards[0].astype(jnp.bfloat16), "context").astype(jnp.float32),
        lax.psum(shards[1].astype(jnp.bfloat16), "context").astype(jnp.float32),
        lax.psum(shards[2].astype(jnp.bfloat16), "context").astype(jnp.float32),
        lax.psum(shards[3].astype(jnp.bfloat16), "context").astype(jnp.float32),
        lax.psum(shards[4].astype(jnp.bfloat16), "context").astype(jnp.float32),
        lax.psum(shards[5].astype(jnp.bfloat16), "context").astype(jnp.float32),
    )
    return (result, grad_input, owned[0], owned[1], owned[2], owned[3], owned[4], owned[5])


def solution(mesh):
    return jax.shard_map(
        per_device,
        mesh=mesh,
        in_specs=(
            P("dp", ("context", "tensor"), None),
            P("dp", None),
            P("dp", None, "tensor"),
            P("tensor", "dp"),
            P("dp", "tensor"),
            P("tensor", "dp"),
            P("dp"),
            P("dp"),
            P("dp", ("context", "tensor"), None),
        ),
        out_specs=(
            P("dp", ("context", "tensor"), None),
            P("dp", ("context", "tensor"), None),
            P("dp", None, "tensor"),
            P("tensor", "dp"),
            P("dp", "tensor"),
            P("tensor", "dp"),
            P("dp"),
            P("dp"),
        ),
        check_vma=False,
    )
```

profile of v0, /device:TPU:1, one launch (start us, length us, event | category | flops | bytes accessed | tf_op | source)
XLA Modules:
  0.0 1330.6 jit_solution(9471987417407896635)
XLA Ops:
  28.5 20.1 %all_gather.32 = bf16[768,3,192]{2,0,1:T(8,128)(2,1)S(1)} all-gather(bf16[192,3,192]{2,0,1:T(8,128)(2,1)S(1)} %copy-done.19), channel_id=1, replica_groups=mesh['dp'=4,'context'=2,'tensor'=4] {'dp'}, dimensions={0}, use_global_device_ids=true | all-gather | bytes 1105920 | tf_op jit(solution)/shard_map/all_gather | solution.py:53
  49.3 36.7 %all-gather.7.cloned.1.call-done = bf16[3,1024,768]{2,1,0:T(8,128)(2,1)} async-done(((bf16[3,256,768]{2,1,0:T(8,128)(2,1)}), bf16[3,1024,768]{2,1,0:T(8,128)(2,1)}) %all-gather.7.cloned.1.call-update) | async-done | bytes 4718608 | tf_op jit(solution)/shard_map/all_gather | solution.py:73
  111.8 12.4 all_gather.33
  148.2 257.0 %while.75 = (s32[]{:T(128)}, bf16[6,512,3,64]{1,3,2,0:T(8,128)(2,1)S(1)}, f32[6,3,512]{2,1,0:T(4,128)}, s32[6]{0:T(128)S(1)}, bf16[3,2048,2,3,64]{1,4,3,2,0:T(8,...) while((s32[]{:T(128)}, ...), condition=%wide.region_4.7_spmd, body=%wide.region_1.6_spmd.sunk | while | flops 850533888 | bytes 47229508 | solution.py:134
  155.9 11.8 gather_fusion
  198.6 11.8 gather_fusion
  241.4 11.8 gather_fusion
  284.1 11.8 gather_fusion
  326.9 11.8 gather_fusion
  418.7 60.2 %reduce-scatter.11.cloned.1.call-done = bf16[3,256,768]{2,1,0:T(8,128)(2,1)} async-done(((bf16[3,1024,768]{2,1,0:T(8,128)(2,1)}), bf16[3,256,768]{2,1,0:T(8,128)(2,1)}) %reduce-scatter.11.cloned.1.call-update) | async-done | bytes 1179664 | tf_op jit(solution)/shard_map/reduce_scatter | solution.py:81
  482.5 40.6 %all-gather.15.cloned.1.call-done = bf16[3,1024,768]{2,1,0:T(8,128)(2,1)} async-done(((bf16[3,256,768]{2,1,0:T(8,128)(2,1)}), bf16[3,1024,768]{2,1,0:T(8,128)(2,1)}) %all-gather.15.cloned.1.call-update) | async-done | bytes 4718608 | tf_op jit(solution)/shard_map/all_gather | solution.py:73
  533.3 21.0 %all-gather.11.cloned.1.call-done = bf16[768,768]{1,0:T(8,128)(2,1)} async-done(((bf16[192,768]{1,0:T(8,128)(2,1)}), bf16[768,768]{1,0:T(8,128)(2,1)}) %all-gather.11.cloned.1.call-update) | async-done | bytes 1179664 | tf_op jit(solution)/shard_map/all_gather | solution.py:55
  554.3 59.1 %all-gather.9.cloned.1.call-done = bf16[3,1024,768]{2,1,0:T(8,128)(2,1)} async-done(((bf16[3,256,768]{2,1,0:T(8,128)(2,1)}), bf16[3,1024,768]{2,1,0:T(8,128)(2,1)}) %all-gather.9.cloned.1.call-update) | async-done | bytes 4718608 | tf_op jit(solution)/shard_map/all_gather | solution.py:73
  613.3 16.2 %fusion.48 = (bf16[3072,768]{1,0:T(8,128)(2,1)S(1)}, f32[3072,768]{1,0:T(8,128)}) fusion(f32[3072,768]{1,0:T(8,128)} %fusion.69, bf16[3072,768]{1,0:T(8,128)(2,1)} %bitcast.218, bf16[768,768]{1,0:T(8,128)(2,1)} %all-gather.11.cloned.1.call-done), kind=kOutput, calls=%fused_computation.89 | convolution fusion | flops 3671064576 | bytes 29491200 | tf_op jit(solution)/shard_map/dot_general | solution.py:146
  635.1 57.3 %reduce-scatter.15.cloned.1.call-done = bf16[3,256,768]{2,1,0:T(8,128)(2,1)} async-done(((bf16[3,1024,768]{2,1,0:T(8,128)(2,1)}), bf16[3,256,768]{2,1,0:T(8,128)(2,1)}) %reduce-scatter.15.cloned.1.call-update) | async-done | bytes 1179664 | tf_op jit(solution)/shard_map/reduce_scatter | solution.py:76
  700.2 54.8 %all-gather.17.cloned.1.call-done = bf16[3,1024,768]{2,1,0:T(8,128)(2,1)} async-done(((bf16[3,256,768]{2,1,0:T(8,128)(2,1)}), bf16[3,1024,768]{2,1,0:T(8,128)(2,1)}) %all-gather.17.cloned.1.call-update) | async-done | bytes 4718608 | tf_op jit(solution)/shard_map/all_gather | solution.py:73
  776.1 327.5 %while.77 = (s32[]{:T(128)}, bf16[3,1024,3,64]{1,3,2,0:T(8,128)(2,1)}, f32[3,2048,2,3,64]{1,4,3,2,0:T(8,128)}, s32[3]{0:T(128)}, bf16[3,1024,3,64]{1,3,2,0:T(8,1...) while((s32[]{:T(128)}, ...), condition=%wide.region_14.17_spmd, body=%wide.region_10.16_spmd.sunk | while | flops 2055052800 | bytes 127489152 | solution.py:225
  778.4 100.6 %while.78 = (s32[]{:T(128)}, f32[2048,2,3,64]{0,3,2,1:T(8,128)S(1)}, bf16[2,512,3,64]{1,3,2,0:T(8,128)(2,1)}, s32[2]{0:T(128)S(1)}, s32[]{:T(128)}, /*index=5*/b...) while((s32[]{:T(128)}, ...), condition=%wide.region_13.15_spmd.clone, body=%wide.region_11.14_spmd.clone.sunk | while | flops 2055052800 | bytes 118837976 | solution.py:220
  784.5 11.8 gather_fusion.2
  887.4 100.6 %while.78 = (s32[]{:T(128)}, f32[2048,2,3,64]{0,3,2,1:T(8,128)S(1)}, bf16[2,512,3,64]{1,3,2,0:T(8,128)(2,1)}, s32[2]{0:T(128)S(1)}, s32[]{:T(128)}, /*index=5*/b...) while((s32[]{:T(128)}, ...), condition=%wide.region_13.15_spmd.clone, body=%wide.region_11.14_spmd.clone.sunk | while | flops 2055052800 | bytes 118837976 | solution.py:220
  996.4 100.6 %while.78 = (s32[]{:T(128)}, f32[2048,2,3,64]{0,3,2,1:T(8,128)S(1)}, bf16[2,512,3,64]{1,3,2,0:T(8,128)(2,1)}, s32[2]{0:T(128)S(1)}, s32[]{:T(128)}, /*index=5*/b...) while((s32[]{:T(128)}, ...), condition=%wide.region_13.15_spmd.clone, body=%wide.region_11.14_spmd.clone.sunk | while | flops 2055052800 | bytes 118837976 | solution.py:220
  1148.4 30.1 %reduce-scatter.19.cloned.1.call-done = bf16[192,3,192]{2,0,1:T(8,128)(2,1)} async-done(((bf16[768,3,192]{2,0,1:T(8,128)(2,1)}), bf16[192,3,192]{2,0,1:T(8,128)(2,1)}) %reduce-scatter.19.cloned.1.call-update) | async-done | bytes 221200 | tf_op jit(solution)/shard_map/reduce_scatter | solution.py:249
  1204.8 53.5 %reduce-scatter.17.cloned.1.call-done = bf16[3,256,768]{2,1,0:T(8,128)(2,1)} async-done(((bf16[3,1024,768]{2,1,0:T(8,128)(2,1)}), bf16[3,256,768]{2,1,0:T(8,128)(2,1)}) %reduce-scatter.17.cloned.1.call-update) | async-done | bytes 1179664 | tf_op jit(solution)/shard_map/reduce_scatter | solution.py:76
  1293.3 25.0 %reduce-scatter.13.cloned.1.call-done = bf16[3,256,768]{2,1,0:T(8,128)(2,1)} async-done(((bf16[3,1024,768]{2,1,0:T(8,128)(2,1)}), bf16[3,256,768]{2,1,0:T(8,128)(2,1)}) %reduce-scatter.13.cloned.1.call-update) | async-done | bytes 1179664 | tf_op jit(solution)/shard_map/reduce_scatter | solution.py:81
  (441 shorter events, 730.1 us)
Async XLA Ops:
  8.0 78.0 %all-gather.7.cloned.1.call-start = ((), (), s32[]{:S(2)}) async-start(), calls=%async_computation.8 | async-start | bytes 5898240 | tf_op jit(solution)/shard_map/all_gather | solution.py:73
  28.5 450.5 %reduce-scatter.11.cloned.1.call-start = ((), (), s32[]{:S(2)}) async-start(), calls=%async_computation.9 | async-start | bytes 5898240 | tf_op jit(solution)/shard_map/reduce_scatter | solution.py:81
  110.2 14.5 %collective-permute-start = (bf16[3,1024,2,192]{1,3,2,0:T(8,128)(2,1)}, bf16[3,1024,2,192]{1,3,2,0:T(8,128)(2,1)}, u32[]{:S(2)}, u32[]{:S(2)}) collective-permute-start(bf16[3,1024,2,192]{1,3,2,0:T(8,128)(2,1)} %copy.38), channel_id=1, source_target_pairs={{0,4},{1,5},{2,6},{3,7},{8,12},{9,13},{10,14},{11,15},{16,20},{17,... | collective-permute-start | bytes 7077896 | tf_op jit(solution)/shard_map/ppermute | solution.py:19
  416.9 62.1 %copy-start = (bf16[3,256,768]{2,1,0:T(8,128)(2,1)S(1)}, bf16[3,256,768]{2,1,0:T(8,128)(2,1)}, u32[]{:S(2)}) copy-start(bf16[3,256,768]{2,1,0:T(8,128)(2,1)} %param.19) | copy-start | bytes 3538948
  416.9 65.6 %all-gather.13.cloned.1.call-start = ((), (), s32[]{:S(2)}) async-start(), calls=%async_computation.12 | async-start | bytes 1474560 | tf_op jit(solution)/shard_map/all_gather | solution.py:56
  417.5 105.6 %all-gather.15.cloned.1.call-start = ((), (), s32[]{:S(2)}) async-start(), calls=%async_computation.14 | async-start | bytes 5898240 | tf_op jit(solution)/shard_map/all_gather | solution.py:73
  418.1 136.2 %all-gather.11.cloned.1.call-start = ((), (), s32[]{:S(2)}) async-start(), calls=%async_computation.11 | async-start | bytes 1474560 | tf_op jit(solution)/shard_map/all_gather | solution.py:55
  418.7 194.7 %all-gather.9.cloned.1.call-start = ((), (), s32[]{:S(2)}) async-start(), calls=%async_computation.10 | async-start | bytes 5898240 | tf_op jit(solution)/shard_map/all_gather | solution.py:73
  418.7 276.8 %copy-start.20 = (f32[768]{0:T(1024)}, f32[768]{0:T(1024)S(1)}, u32[]{:S(2)}) copy-start(f32[768]{0:T(1024)S(1)} %convert_element_type.177) | copy-start | bytes 9220
  480.8 214.7 %copy-start.22 = (f32[3,256]{1,0:T(4,128)}, f32[3,256]{1,0:T(4,128)S(1)}, u32[]{:S(2)}) copy-start(f32[3,256]{1,0:T(4,128)S(1)} %fusion.67) | copy-start | bytes 9220
  482.3 210.1 %reduce-scatter.15.cloned.1.call-start = ((), (), s32[]{:S(2)}) async-start(), calls=%async_computation.15 | async-start | bytes 5898240 | tf_op jit(solution)/shard_map/reduce_scatter | solution.py:76
  635.0 120.0 %all-gather.17.cloned.1.call-start = ((), (), s32[]{:S(2)}) async-start(), calls=%async_computation.16 | async-start | bytes 5898240 | tf_op jit(solution)/shard_map/all_gather | solution.py:73
  698.1 436.9 %reduce-scatter.25.cloned.1.call-start = ((), (), s32[]{:S(2)}) async-start(), calls=%async_computation.21 | async-start | bytes 491520
  759.4 377.3 %reduce-scatter.21.cloned.1.call-start = ((), (), s32[]{:S(2)}) async-start(), calls=%async_computation.19 | async-start | bytes 1474560 | tf_op jit(solution)/shard_map/reduce_scatter | solution.py:255
  768.2 380.2 %reduce-scatter.23.cloned.1.call-start = ((), (), s32[]{:S(2)}) async-start(), calls=%async_computation.20 | async-start | bytes 1474560 | tf_op jit(solution)/shard_map/reduce_scatter | solution.py:258
  1106.5 13.6 %collective-permute-start.1 = (bf16[3,1024,2,3,64]{1,4,3,2,0:T(8,128)(2,1)S(1)}, bf16[3,1024,2,3,64]{1,4,3,2,0:T(8,128)(2,1)}, u32[]{:S(2)}, u32[]{:S(2)}) collective-permute-start(bf16[3,1024,2,3,64]{1,4,3,2,0:T(8,128)(2,1)S(1)} %slice.81), channel_id=1, source_target_pairs={{4,0},{5,1},{6,2},{7,3},{12,8},{13,9},{14,10},{15,11},{20,16},{21,... | collective-permute-start | bytes 7077896 | tf_op jit(solution)/shard_map/ppermute | solution.py:19
  1120.0 58.5 %reduce-scatter.19.cloned.1.call-start = ((), (), s32[]{:S(2)}) async-start(), calls=%async_computation.18 | async-start | bytes 1474560 | tf_op jit(solution)/shard_map/reduce_scatter | solution.py:249
  1134.9 62.7 %all-reduce.11.cloned.1.call-start = ((), (), s32[]{:S(2)}) async-start(), calls=%async_computation.22 | async-start | bytes 1966080 | tf_op jit(solution)/shard_map/psum | solution.py:269
  1178.5 79.8 %reduce-scatter.17.cloned.1.call-start = ((), (), s32[]{:S(2)}) async-start(), calls=%async_computation.17 | async-start | bytes 5898240 | tf_op jit(solution)/shard_map/reduce_scatter | solution.py:76
  1185.8 132.5 %reduce-scatter.13.cloned.1.call-start = ((), (), s32[]{:S(2)}) async-start(), calls=%async_computation.13 | async-start | bytes 5898240 | tf_op jit(solution)/shard_map/reduce_scatter | solution.py:81
  1196.8 121.6 %copy-start.4 = (bf16[3,256,768]{2,1,0:T(8,128)(2,1)S(1)}, bf16[3,256,768]{2,1,0:T(8,128)(2,1)}, u32[]{:S(2)}) copy-start(bf16[3,256,768]{2,1,0:T(8,128)(2,1)} %reduce-scatter.11.cloned.1.call-done) | copy-start | bytes 3538948
  1196.8 121.6 %copy-start.8 = (bf16[3,256,768]{2,1,0:T(8,128)(2,1)S(1)}, bf16[3,256,768]{2,1,0:T(8,128)(2,1)}, u32[]{:S(2)}) copy-start(bf16[3,256,768]{2,1,0:T(8,128)(2,1)} %reduce-scatter.15.cloned.1.call-done) | copy-start | bytes 3538948
  1196.8 121.6 %copy-start.21 = (f32[768]{0:T(1024)S(1)}, f32[768]{0:T(1024)}, u32[]{:S(2)}) copy-start(f32[768]{0:T(1024)} %copy-done.20) | copy-start | bytes 9220
  1196.8 121.6 %copy-start.23 = (f32[3,256]{1,0:T(4,128)S(1)}, f32[3,256]{1,0:T(4,128)}, u32[]{:S(2)}) copy-start(f32[3,256]{1,0:T(4,128)} %copy-done.22) | copy-start | bytes 9220
  (42 other events, 525.0 us)
Sparse Core Ops, SparseCore 0:
  28.6 57.3 all-gather.6
  417.0 61.8 reduce-scatter.10
  635.2 57.1 reduce-scatter.14
  1178.7 18.9 all-reduce.10
  1200.5 57.8 reduce-scatter.16
  1261.2 57.1 reduce-scatter.12
Sparse Core Ops, SparseCore 1:
  418.9 34.4 all-gather.12
  455.1 68.0 all-gather.14
  524.5 29.7 all-gather.10
  556.7 56.6 all-gather.8
  698.2 56.8 all-gather.16
  759.4 18.7 reduce-scatter.24
  780.5 28.8 reduce-scatter.20
  1120.1 28.3 reduce-scatter.22
  1150.7 27.8 reduce-scatter.18
where the time goes:
time: 1340 us; the launch traced here: 1330 us
  waiting for transfers between devices  452 us (34%)
  local copies, waits for them, and re-layouts  305 us (23%)
  matrix products  303 us (23%)
  other arithmetic  152 us (11%)
  blocking collectives  69.5 us (5%)
  loops' own time  24.9 us (2%)
  between operations  18 us (1%)
    all_gather x4, waiting for transfers between devices, gather_rows(): return lax.all_gather(values, 'tensor', axis=1, tiled=True)  191 us
    gather x12, local copies, waits for them, and re-layouts, block_setup(): key_seg = jnp.take(segrow, jnp.clip(key_pos, 0, total_len - 1))  141 us
    reduce_scatter x2, waiting for transfers between devices, scatter_rows(): lax.psum_scatter(values.astype(jnp.bfloat16), 'tensor', scatter_dimension...  111 us
    dot_general x12, matrix products, block_setup(): jnp.einsum('qhd,khd->hqk', query_block, keyval_block[:, 0], preferred_ele...  91.6 us
    reduce_scatter x2, waiting for transfers between devices, branch_reduce(): lax.psum_scatter(values.astype(jnp.bfloat16), 'tensor', scatter_dimension...  85.3 us
    reduce_sum x6, other arithmetic, forward_block(): denominator = jnp.sum(exponent, axis=-1, keepdims=True)  40.6 us
    dot_general x6, matrix products, forward_block(): jnp.einsum('hqk,khd->qhd', soft_low, keyval_block[:, 1], preferred_elemen...  40.6 us
    gather x12, local copies, waits for them, and re-layouts, block_setup(): query_seg = jnp.take(segrow, query_pos)  37.7 us
  transfers between devices with their start and end apart: 17, of which 11 were waited for; matrix products, arithmetic and copies ran while one was open for 31% of the time, Pallas kernels for 0%

commit v1 on v0

v1 whole, which is shorter than its diff:
```python
import functools
import math

import jax
import jax.numpy as jnp
from jax import lax
from jax.experimental import pallas as pl
from jax.experimental.pallas import tpu as pltpu
from jax.sharding import PartitionSpec as P

HD = 64
WIN = 1536
QB = 256
CHUNK = 128
NEG = -1e30
epsilon = 1e-06
low = jnp.bfloat16
full = jnp.float32


def dot(left, right, dims):
    return lax.dot_general(left, right, (dims, ((), ())), preferred_element_type=full)


def nn(left, right):
    return dot(left, right, ((1,), (0,)))


def nt(left, right):
    return dot(left, right, ((1,), (1,)))


def tn(left, right):
    return dot(left, right, ((0,), (0,)))


def across(array, axis, by):
    return lax.ppermute(array, axis, [(i, i ^ by) for i in range(lax.axis_size(axis))])


def gather_tensor(array, axis):
    half = array.shape[axis] // 2
    one = lax.slice_in_dim(array, 0, half, axis=axis)
    two = lax.slice_in_dim(array, half, 2 * half, axis=axis)
    one_x, two_y = across(one, "tensor", 1), across(two, "tensor", 2)
    one_y, one_d = across(one, "tensor", 2), across(one_x, "tensor", 2)
    two_x, two_d = across(two, "tensor", 1), across(two_y, "tensor", 1)
    join = lambda a, b: jnp.concatenate([a, b], axis=axis)
    return [array, join(one_x, two_x), join(one_y, two_y), join(one_d, two_d)]


def scatter_tensor(parts, axis):
    half = parts[0].shape[axis] // 2
    one = [lax.slice_in_dim(p, 0, half, axis=axis) for p in parts]
    two = [lax.slice_in_dim(p, half, 2 * half, axis=axis) for p in parts]

    def reduce(p, first, second):
        sent = jnp.stack([p[first], p[first ^ second]]).astype(low)
        got = across(sent, "tensor", first).astype(full)
        mine, theirs = p[0] + got[0], p[second] + got[1]
        return mine + across(theirs.astype(low), "tensor", second).astype(full)

    return jnp.concatenate([reduce(one, 1, 2), reduce(two, 2, 1)], axis=axis)


UNITS = 5


def unit_block(part):
    return lambda u, c: (jnp.where(u < 3, part * 3 + u, 9 + part * 2 + (u - 3)), 0, 0)


def attend_kernel(c_ref, qm, km, vm, qt, kt, vt, lo_ref, om, ot, lse_ref, of_ref, qs, ks, vs, ss):
    c = c_ref[0]
    length = lo_ref.shape[2]
    half = length // 2
    for place, q, k, v in ((c, qm, km, vm), (1 - c, qt, kt, vt)):
        off = pl.multiple_of(place * half, half)
        qs[:, pl.ds(off, half)] = q[0] * low(0.125)
        vs[:, pl.ds(off, half)] = v[0]
        ks[pl.ds(off, half), :] = k[0].T
    for start in range(0, length, QB):
        stop = start + QB
        q = qs[:, start:stop]
        lo = lo_ref[0, :, start:stop]
        first = max(0, start - WIN)
        most = jnp.full((8, QB), NEG, full)
        for at in range(first, stop, CHUNK):
            s = nn(ks[at : at + CHUNK, :], q)
            key_pos = at + lax.broadcasted_iota(jnp.int32, (CHUNK, QB), 0)
            allowed = key_pos >= lo
            if at + CHUNK - 1 > start:
                allowed &= key_pos <= start + lax.broadcasted_iota(jnp.int32, (CHUNK, QB), 1)
            s = jnp.where(allowed, s, NEG)
            ss[at - first : at - first + CHUNK, :] = s
            most = jnp.maximum(most, jnp.max(s.reshape(CHUNK // 8, 8, QB), axis=0))
        most = jnp.max(most, axis=0, keepdims=True)
        total = jnp.zeros((8, QB), full)
        acc = jnp.zeros((HD, QB), full)
        for at in range(first, stop, CHUNK):
            p = jnp.exp(ss[at - first : at - first + CHUNK, :] - most)
            total += jnp.sum(p.reshape(CHUNK // 8, 8, QB), axis=0)
            acc += nn(vs[:, at : at + CHUNK], p.astype(low))
        total = jnp.sum(total, axis=0, keepdims=True)
        lse_ref[0, :, start:stop] = most + jnp.log(total)
        of_ref[0, :, start:stop] = acc * (1.0 / total)
    om[0] = of_ref[0, :, pl.ds(pl.multiple_of(c * half, half), half)].astype(low)
    ot[0] = of_ref[0, :, pl.ds(pl.multiple_of((1 - c) * half, half), half)].astype(low)


def attend(c, mine, theirs, lo):
    length = lo.shape[2]
    half = length // 2
    part = lambda p: pl.BlockSpec((1, HD, half), unit_block(p))
    unit = lambda rows, n: pl.BlockSpec((1, rows, n), lambda u, c: (u, 0, 0))
    return pl.pallas_call(
        attend_kernel,
        grid_spec=pltpu.PrefetchScalarGridSpec(
            num_scalar_prefetch=1,
            grid=(UNITS,),
            in_specs=[part(0), part(1), part(2)] * 2
            + [pl.BlockSpec((1, 1, length), lambda u, c: (u // 3, 0, 0))],
            out_specs=[unit(HD, half), unit(HD, half), unit(1, length), unit(HD, length)],
            scratch_shapes=[
                pltpu.VMEM((HD, length), low),
                pltpu.VMEM((length, HD), low),
                pltpu.VMEM((HD, length), low),
                pltpu.VMEM((WIN + QB, QB), full),
            ],
        ),
        out_shape=[jax.ShapeDtypeStruct((UNITS, HD, half), low)] * 2
        + [
            jax.ShapeDtypeStruct((UNITS, 1, length), full),
            jax.ShapeDtypeStruct((UNITS, HD, length), full),
        ],
        compiler_params=pltpu.CompilerParams(vmem_limit_bytes=40 << 20),
        cost_estimate=pl.CostEstimate(
            flops=UNITS * 18 * 2 * 256 * 1024 * 128, bytes_accessed=20 << 20, transcendentals=0
        ),
        name="attend",
    )(c, mine, mine, mine, theirs, theirs, theirs, lo)


def attend_back_kernel(
    c_ref, qm, km, vm, gm, qt, kt, vt, gt, lo_ref, lse_ref, of_ref, dm, dt,
    qs, ks, kts, vs, gs, grow, qrow, delta, dqs, dks, dvs,
):
    c = c_ref[0]
    length = lo_ref.shape[2]
    half = length // 2
    for place, q, k, v, g in ((c, qm, km, vm, gm), (1 - c, qt, kt, vt, gt)):
        off = pl.multiple_of(place * half, half)
        scaled = q[0] * low(0.125)
        qs[:, pl.ds(off, half)] = scaled
        kts[:, pl.ds(off, half)] = k[0]
        gs[:, pl.ds(off, half)] = g[0]
        ks[pl.ds(off, half), :] = k[0].T
        vs[pl.ds(off, half), :] = v[0].T
        grow[pl.ds(off, half), :] = g[0].T
        qrow[pl.ds(off, half), :] = scaled.T
        delta[:, pl.ds(off, half)] = jnp.sum(
            g[0].astype(full) * of_ref[0, :, pl.ds(off, half)], axis=0, keepdims=True
        )
    dqs[...] = jnp.zeros_like(dqs)
    for key_start in range(0, length, QB):
        rows = slice(key_start, key_start + QB)
        k, v, key_t = ks[rows, :], vs[rows, :], kts[:, rows]
        dk = jnp.zeros((QB, HD), full)
        dv = jnp.zeros((QB, HD), full)
        key_pos = key_start + lax.broadcasted_iota(jnp.int32, (QB, QB), 0)
        for start in range(key_start, min(key_start + WIN + QB, length), QB):
            cols = slice(start, start + QB)
            s = nn(k, qs[:, cols]) - lse_ref[0, :, cols]
            allowed = key_pos >= lo_ref[0, :, cols]
            if start == key_start:
                allowed &= key_pos <= start + lax.broadcasted_iota(jnp.int32, (QB, QB), 1)
            p = jnp.exp(jnp.where(allowed, s, NEG))
            dp = nn(v, gs[:, cols])
            ds = (p * (dp - delta[:, cols])).astype(low)
            dv += nn(p.astype(low), grow[cols, :])
            dk += nn(ds, qrow[cols, :])
            dqs[:, cols] += nn(key_t, ds)
        dks[:, rows] = dk.T.astype(low)
        dvs[:, rows] = dv.T.astype(low)
    for ref, place in ((dm, c), (dt, 1 - c)):
        off = pl.ds(pl.multiple_of(place * half, half), half)
        ref[0, 0] = (dqs[:, off] * 0.125).astype(low)
        ref[0, 1] = dks[:, off]
        ref[0, 2] = dvs[:, off]


def attend_back(c, mine, theirs, grad_mine, grad_theirs, lo, lse, attended):
    length = lo.shape[2]
    half = length // 2
    part = lambda p: pl.BlockSpec((1, HD, half), unit_block(p))
    unit = lambda rows, n: pl.BlockSpec((1, rows, n), lambda u, c: (u, 0, 0))
    wide, tall = pltpu.VMEM((HD, length), low), pltpu.VMEM((length, HD), low)
    return pl.pallas_call(
        attend_back_kernel,
        grid_spec=pltpu.PrefetchScalarGridSpec(
            num_scalar_prefetch=1,
            grid=(UNITS,),
            in_specs=[part(0), part(1), part(2), unit(HD, half)] * 2
            + [
                pl.BlockSpec((1, 1, length), lambda u, c: (u // 3, 0, 0)),
                unit(1, length),
                unit(HD, length),
            ],
            out_specs=[pl.BlockSpec((1, 3, HD, half), lambda u, c: (u, 0, 0, 0))] * 2,
            scratch_shapes=[
                wide, tall, wide, tall, wide, tall, tall,
                pltpu.VMEM((1, length), full), pltpu.VMEM((HD, length), full), wide, wide,
            ],
        ),
        out_shape=[jax.ShapeDtypeStruct((UNITS, 3, HD, half), low)] * 2,
        compiler_params=pltpu.CompilerParams(vmem_limit_bytes=40 << 20),
        cost_estimate=pl.CostEstimate(
            flops=UNITS * 18 * 5 * 256 * 1024 * 128, bytes_accessed=30 << 20, transcendentals=0
        ),
        name="attend_back",
    )(c, mine, mine, mine, grad_mine, theirs, theirs, theirs, grad_theirs, lo, lse, attended)


def gelu_and_slope(v):
    k0 = math.sqrt(2.0 / math.pi)
    square = v * v
    th = jnp.tanh(k0 * v * (1.0 + 0.044715 * square))
    slope = 0.5 * (1.0 + th) + 0.5 * v * (1.0 - th * th) * k0 * (1.0 + 3.0 * 0.044715 * square)
    return 0.5 * v * (1.0 + th), slope


def per_device(tokens, segments, w_qkv, w_out, w_in, w_back, gain_attn, gain_mlp, cotangent):
    sequences, own, width = tokens.shape
    assert lax.axis_size("tensor") == 4 and lax.axis_size("context") == 2 and sequences == 3
    c, t, d = lax.axis_index("context"), lax.axis_index("tensor"), lax.axis_index("dp")
    span = 4 * own
    length = segments.shape[1]
    shard = w_qkv.shape[0]
    local = w_qkv.shape[2]
    heads = local // HD
    hidden = w_in.shape[1] // 2
    rows = sequences * own

    blocks = gather_tensor(tokens, 1)
    cot_theirs = across(cotangent, "context", 1)
    w_attn = lax.all_gather(w_qkv.reshape(shard, 3 * local), "dp", axis=0, tiled=True)
    gains = lax.all_gather(jnp.stack([gain_attn, gain_mlp], axis=1), "dp", axis=0, tiled=True)
    gain_first, gain_second = gains[:, 0].astype(full), gains[:, 1].astype(full)
    up_own = lax.dynamic_slice_in_dim(w_in, c * hidden, hidden, 1)
    down_own = lax.dynamic_slice_in_dim(w_back, c * hidden, hidden, 0).T
    up_down = jnp.stack(gather_tensor(jnp.stack([up_own, down_own]), 1), axis=1)
    up_down = lax.all_gather(up_down, "dp", axis=2, tiled=True)
    w_up, w_down = up_down[0], up_down[1]
    w_proj = jnp.stack(gather_tensor(w_out.T, 0), axis=0)
    w_proj = lax.all_gather(w_proj, "dp", axis=1, tiled=True)

    lo = jnp.zeros((sequences, length), jnp.int32)
    for value in range(8):
        before = jnp.sum((segments < value).astype(jnp.int32), axis=1, keepdims=True)
        lo = jnp.where(segments == value, before, lo)
    lo = jnp.maximum(lo, jnp.arange(length, dtype=jnp.int32)[None] - (WIN - 1))
    lo = jnp.stack([jnp.where(c == 0, lo[0], lo[2]), lo[1]])[:, None]

    stacked = jnp.stack(blocks)
    in_order = lambda s: [lax.dynamic_index_in_dim(s, t ^ p, 0, False) for p in range(4)]
    all_tokens = jnp.stack(in_order(stacked), axis=1).reshape(sequences * span, width)

    def inverse(v):
        return lax.rsqrt(jnp.mean(v * v, axis=-1, keepdims=True) + epsilon)

    wide_tokens = all_tokens.astype(full)
    normed_one = (wide_tokens * inverse(wide_tokens) * gain_first).astype(low)
    projected = dot(w_attn, normed_one, ((0,), (1,))).astype(low)

    def units(array, parts, core):
        block = array.reshape(parts, heads, HD, sequences * span)
        whole = lax.dynamic_slice_in_dim(block, 2 * core * span, span, 3)
        shared = lax.dynamic_slice_in_dim(block[..., span : 2 * span], core, 2, 1)
        whole, shared = (a.reshape(-1, HD, span) for a in (whole, shared))
        return jnp.concatenate([whole, shared], axis=0)

    def rejoin(mine, theirs):
        first = jnp.where(c == 0, mine[:3], theirs[:3])
        last = jnp.where(c == 0, theirs[:3], mine[:3])
        shared = jnp.where(
            c == 0,
            jnp.concatenate([mine[3:5], theirs[4:5]]),
            jnp.concatenate([theirs[3:4], mine[3:5]]),
        )
        return jnp.stack([first, shared, last])

    core = c.reshape(1).astype(jnp.int32)
    qkv_mine = units(projected, 3, c)
    qkv_theirs = across(units(projected, 3, 1 - c), "context", 1)
    out_mine, out_sent, log_totals, out_full = attend(core, qkv_mine, qkv_theirs, lo)
    heads_out = rejoin(out_mine, across(out_sent, "context", 1))
    heads_out = heads_out.reshape(sequences, local, span)

    def to_owner(array, by):
        piece = lax.dynamic_slice_in_dim(array, (t ^ by) * own, own, 2)
        return across(piece, "tensor", by) if by else piece

    attended = jnp.stack([to_owner(heads_out, r) for r in range(4)])
    attended = attended.transpose(0, 2, 1, 3).reshape(4 * local, rows)

    proj_rows = w_proj.transpose(0, 2, 1).reshape(4 * local, width)
    inputs = tokens.astype(full).reshape(rows, width)
    middle = inputs + tn(attended, proj_rows)
    inv_two = inverse(middle)
    normed_two = (middle * inv_two * gain_second).astype(low)

    both = jnp.concatenate([normed_two, across(normed_two, "context", 1)], axis=0)
    cot = cotangent.reshape(rows, width)
    both_cot = jnp.concatenate([cot, cot_theirs.reshape(rows, width)], axis=0)
    up = w_up.transpose(1, 0, 2).reshape(width, 4 * hidden)
    down = w_down.transpose(1, 0, 2).reshape(width, 4 * hidden)
    hidden_pre = nn(both, up)
    active, slope = gelu_and_slope(hidden_pre)
    active = active.astype(low)
    grad_hidden = (nn(both_cot, down) * slope).astype(low)
    branch = nt(active, down)
    back = nt(grad_hidden, up)
    crossed = across(back[rows:].astype(low), "context", 1).astype(full)
    grad_norm_two = back[:rows] + crossed
    crossed = across(branch[rows:].astype(low), "context", 1).astype(full)
    result = (middle + branch[:rows] + crossed).astype(low)
    grad_down = tn(both_cot, active)
    grad_up = tn(both, grad_hidden)

    def norm_back(r, gain, v, inv):
        rg = r * gain
        return inv * (rg - v * (inv * inv * jnp.mean(rg * v, axis=-1, keepdims=True)))

    grad_middle = cot.astype(full) + norm_back(grad_norm_two, gain_second, middle, inv_two)
    grad_low = grad_middle.astype(low)
    grad_proj = nn(attended, grad_low)
    grad_att = nt(proj_rows, grad_low).astype(low).reshape(4, local, sequences, own)
    grad_heads = jnp.stack([across(grad_att[r], "tensor", r) if r else grad_att[0] for r in range(4)])
    grad_heads = jnp.stack(in_order(grad_heads), axis=2).reshape(local, sequences * span)
    g_mine = units(grad_heads, 1, c)
    g_theirs = across(units(grad_heads, 1, 1 - c), "context", 1)
    d_mine, d_sent = attend_back(core, qkv_mine, qkv_theirs, g_mine, g_theirs, lo, log_totals, out_full)
    grad_projected = rejoin(d_mine, across(d_sent, "context", 1))
    grad_projected = grad_projected.transpose(2, 1, 3, 0, 4).reshape(3 * local, sequences * span)
    grad_attn = nn(grad_projected, normed_one)
    spread = dot(grad_projected, w_attn, ((0,), (1,))).reshape(sequences, 4, own, width)
    spread = [lax.dynamic_index_in_dim(spread, t ^ r, 1, False) for r in range(4)]
    grad_norm_one = scatter_tensor(spread, 1).reshape(rows, width)
    inv_one = inverse(inputs)
    grad_input = grad_middle + norm_back(grad_norm_one, gain_first, inputs, inv_one)

    def scatter_dp(array, axis):
        return lax.psum_scatter(array.astype(low), "dp", scatter_dimension=axis, tiled=True)

    def swap_halves(mine, axis):
        theirs = across(mine, "context", 1)
        return jnp.where(
            c == 0,
            jnp.concatenate([mine, theirs], axis=axis),
            jnp.concatenate([theirs, mine], axis=axis),
        )

    def half_sum(array, axis):
        size = array.shape[axis] // 2
        mine = lax.dynamic_slice_in_dim(array, c * size, size, axis)
        sent = lax.dynamic_slice_in_dim(array, (1 - c) * size, size, axis)
        return mine + across(sent.astype(low), "context", 1).astype(full)

    up_down = jnp.stack([grad_up, grad_down]).reshape(2, width, 4, hidden)
    up_down = scatter_tensor([up_down[:, :, r] for r in range(4)], 1)
    up_down = scatter_dp(up_down, 1)
    own_up = swap_halves(up_down[0], 1).astype(full)
    own_down = swap_halves(up_down[1].T, 0).astype(full)
    proj = half_sum(grad_proj.reshape(4, local, width), 1)
    proj = scatter_dp(scatter_tensor([proj[r] for r in range(4)], 0), 1)
    own_proj = swap_halves(proj, 0).astype(full)
    attn = scatter_dp(half_sum(grad_attn, 0), 1).T
    own_attn = swap_halves(attn, 1).astype(full)

    def gain_grad(weight, grad, gain):
        part = jnp.sum(weight.astype(full) * grad, axis=1)
        return lax.psum(part, "tensor") / gain.astype(full)

    own_gain_attn = gain_grad(w_qkv.reshape(shard, 3 * local), own_attn, gain_attn)
    own_gain_mlp = gain_grad(w_in, own_up, gain_mlp)
    return (
        result.reshape(sequences, own, width),
        grad_input.astype(low).reshape(sequences, own, width),
        own_attn.reshape(shard, 3, local),
        own_proj,
        own_up,
        own_down,
        own_gain_attn,
        own_gain_mlp,
    )


def solution(mesh):
    return jax.shard_map(
        per_device,
        mesh=mesh,
        in_specs=(
            P("dp", ("context", "tensor"), None),
            P("dp", None),
            P("dp", None, "tensor"),
            P("tensor", "dp"),
            P("dp", "tensor"),
            P("tensor", "dp"),
            P("dp"),
            P("dp"),
            P("dp", ("context", "tensor"), None),
        ),
        out_specs=(
            P("dp", ("context", "tensor"), None),
            P("dp", ("context", "tensor"), None),
            P("dp", None, "tensor"),
            P("tensor", "dp"),
            P("dp", "tensor"),
            P("tensor", "dp"),
            P("dp"),
            P("dp"),
        ),
        check_vma=False,
    )
```

time: 1340 us -> 518 us (0.39)
  waiting for transfers between devices: 452 us -> 89.9 us
  matrix products: 303 us -> 67.2 us
  local copies, waits for them, and re-layouts: 305 us -> 99.9 us
  other arithmetic: 152 us -> 65.8 us
  Pallas kernels: 0 us -> 67 us
  starting transfers between devices: 6.75 us -> 55.7 us
  loops' own time: 24.9 us -> 0 us
  blocking collectives: 69.5 us -> 51.3 us
    reduce_scatter x7 -> x1, waiting for transfers between devices: 238 us -> 0.02 us  [scatter_dp(): lax.psum_scatter(array.astype(low), 'dp', scatter_dimension=axis, tiled=T...]
    dot_general x54 -> x12, matrix products: 303 us -> 67.2 us  [dot(): lax.dot_general(left, right, (dims, ((), ())), preferred_element_type=full)]
    all_gather x6 -> x2, waiting for transfers between devices: 212 us -> 0.01 us  [the longest x1 0.01 us: per_device(): w_proj = lax.all_gather(w_proj, 'dp', axis=1, tiled=True)]
    gather x24 -> x0, local copies, waits for them, and re-layouts: 179 us -> none  [the longest x12 141 us: block_setup(): key_seg = jnp.take(segrow, jnp.clip(key_pos, 0, total_len - 1))]
    ppermute x2 -> x50, waiting for transfers between devices: 0.01 us -> 79.2 us  [across(): lax.ppermute(array, axis, [(i, i ^ by) for i in range(lax.axis_size(axis))])]
    pallas_call x0 -> x2, Pallas kernels: none -> 67 us  [the longest x1 44.4 us: attend_back(): pl.pallas_call(attend_back_kernel, grid_spec=pltpu.PrefetchScalarGridSpec...]
    ppermute x2 -> x50, starting transfers between devices: 5.52 us -> 55 us  [across(): lax.ppermute(array, axis, [(i, i ^ by) for i in range(lax.axis_size(axis))])]
    reduce_sum x10 -> x6, other arithmetic: 50.1 us -> 4.79 us  [the longest x2 3.02 us: inverse(): return lax.rsqrt(jnp.mean(v * v, axis=-1, keepdims=True) + epsilon)]
  transfers between devices with their start and end apart: 17 -> 55, of which waited for: 11 -> 20; matrix products, arithmetic and copies ran while one was open for 31% -> 31% of each run, Pallas kernels for 0% -> 13%
where the time goes in v1:
time: 518 us; the launch traced here: 512 us
  local copies, waits for them, and re-layouts  99.9 us (19%)
  waiting for transfers between devices  89.9 us (17%)
  matrix products  67.2 us (13%)
  Pallas kernels  67 us (13%)
  other arithmetic  65.8 us (13%)
  starting transfers between devices  55.7 us (11%)
  blocking collectives  51.3 us (10%)
  between operations  15.4 us (3%)
    ppermute x50, waiting for transfers between devices, across(): lax.ppermute(array, axis, [(i, i ^ by) for i in range(lax.axis_size(axis))])  79.2 us
    dot_general x12, matrix products, dot(): lax.dot_general(left, right, (dims, ((), ())), preferred_element_type=full)  67.2 us
    ppermute x50, starting transfers between devices, across(): lax.ppermute(array, axis, [(i, i ^ by) for i in range(lax.axis_size(axis))])  55 us
    pallas_call x1, Pallas kernels, attend_back(): pl.pallas_call(attend_back_kernel, grid_spec=pltpu.PrefetchScalarGridSpec...  44.4 us
    all_gather x1, blocking collectives, per_device(): lax.all_gather(w_qkv.reshape(shard, 3 * local), 'dp', axis=0, tiled=True)  34.5 us
    unnamed x144, local copies, waits for them, and re-layouts  29.9 us
    pallas_call x1, Pallas kernels, attend(): pl.pallas_call(attend_kernel, grid_spec=pltpu.PrefetchScalarGridSpec(num_...  22.7 us
    another operation x3, local copies, waits for them, and re-layouts, per_device(): up_down = jnp.stack([grad_up, grad_down]).reshape(2, width, 4, hidden)  13.2 us
  transfers between devices with their start and end apart: 55, of which 20 were waited for; matrix products, arithmetic and copies ran while one was open for 31% of the time, Pallas kernels for 13%

profile of v1, /device:TPU:1, one launch (start us, length us, event | category | flops | bytes accessed | tf_op | source)
XLA Modules:
  0.0 512.2 jit_solution(16182954802605456048)
XLA Ops:
  24.8 34.5 %all_gather.13 = bf16[768,576]{1,0:T(8,128)(2,1)S(1)} all-gather(bf16[192,576]{1,0:T(8,128)(2,1)S(1)} %copy.93), channel_id=1, replica_groups=mesh['dp'=4,'context'=2,'tensor'=4] {'dp'}, dimensions={0}, use_global_device_ids=true | all-gather | bytes 1105920 | tf_op jit(solution)/shard_map/all_gather | solution.py:246
  59.6 10.0 %all-gather = bf16[4,192,2]{1,2,0:T(2,128)(2,1)S(1)} all-gather(bf16[1,192,2]{1,2,0:T(2,128)(2,1)S(1)} %maximum_bitcast_fusion.10), channel_id=1, replica_groups=mesh['dp'=4,'context'=2,'tensor'=4] {'dp'}, dimensions={0}, use_global_device_ids=true | all-gather | bytes 3840 | tf_op jit(solution)/shard_map/all_gather | solution.py:247
  75.2 6.9 %collective-permute-done.23 = bf16[2,96,384]{2,1,0:T(8,128)(2,1)S(1)} collective-permute-done((bf16[2,96,384]{2,1,0:T(8,128)(2,1)S(1)}, bf16[2,96,384]{2,1,0:T(8,128)(2,1)S(1)}, u32[]{:S(2)}, u32[]{:S(2)}) %collective-permute-start.23) | collective-permute-done | bytes 147488 | tf_op jit(solution)/shard_map/ppermute | solution.py:38
  109.3 8.6 %collective-permute-start.6 = (bf16[15,64,1024]{2,1,0:T(8,128)(2,1)}, bf16[15,64,1024]{2,1,0:T(8,128)(2,1)S(1)}, u32[]{:S(2)}, u32[]{:S(2)}) collective-permute-start(bf16[15,64,1024]{2,1,0:T(8,128)(2,1)} %pad_maximum_fusion.5), channel_id=1, source_target_pairs={{0,4},{4,0},{1,5},{5,1},{2,6},{6,2},{3,7},{7,3},{8,12},{12,8},{9,1... | collective-permute-start | bytes 5898248 | tf_op jit(solution)/shard_map/ppermute | solution.py:38
  124.6 22.7 %attend.1 = (bf16[5,64,1024]{2,1,0:T(8,128)(2,1)S(1)}, bf16[5,64,1024]{2,1,0:T(8,128)(2,1)S(1)}, f32[5,1,2048]{2,1,0:T(1,128)S(1)}, f32[5,64,2048]{2,1,0:T(8,128)S(1)}) custom-call(s32[1]{0:T(128)} %bitcast.1.c_ref, bf16[15,64,1024]{2,1,0:T(8,128)(2,1)S(1)} %pad_maximum_fusion.4.qm.km.vm, bf16[15,64,1024]{2,1,0:T(8,128)(2,1)S(1)} %pad_maximum_fusion.4.qm.km.vm, ...), custom_call_target="tpu_custom_call" | custom-call | flops 6039797760 | bytes 20971520 | tf_op jit(solution)/shard_map/attend/pallas_call | solution.py:116
  168.8 9.1 %collective-permute-done.9 = bf16[3,192,256]{2,0,1:T(4,128)(2,1)S(1)} collective-permute-done((bf16[3,192,256]{2,0,1:T(4,128)(2,1)}, bf16[3,192,256]{2,0,1:T(4,128)(2,1)S(1)}, u32[]{:S(2)}, u32[]{:S(2)}) %collective-permute-start.9) | collective-permute-done | bytes 294944 | tf_op jit(solution)/shard_map/ppermute | solution.py:38
  188.2 5.4 %fusion.72 = (bf16[1,4,768,384]{3,1,0,2:T(4,128)(2,1)}, bf16[1,4,768,384]{3,1,0,2:T(4,128)(2,1)S(1)}) fusion(bf16[2,4,768,384]{3,1,0,2:T(4,128)(2,1)} %all-gather.6.cloned.1.call-done), kind=kLoop, calls=%fused_computation.232 | loop fusion | bytes 9437184 | tf_op jit(solution)/shard_map/slice | solution.py:253
  202.9 6.4 %fusion.16 = f32[1536,1536]{1,0:T(8,128)S(1)} fusion(bf16[768,1536]{0,1:T(8,128)(2,1)} %bitcast.305, bf16[768,768]{1,0:T(8,128)(2,1)} %collective-permute-done.17, bf16[768,768]{1,0:T(8,128)(2,1)} %multiply_convert_fusion.2), kind=kOutput, calls=%fused_computation.58 | convolution fusion | flops 3628597248 | bytes 14155776 | tf_op jit(solution)/shard_map/dot_general | solution.py:22
  209.4 7.4 %fusion.69 = f32[1536,768]{1,0:T(8,128)} fusion(bf16[768,1536]{0,1:T(8,128)(2,1)S(1)} %bitcast.307, f32[1536,1536]{1,0:T(8,128)S(1)} %fusion.16), kind=kOutput, calls=%fused_computation.230 | convolution fusion | flops 3645112320 | bytes 16515072 | tf_op jit(solution)/shard_map/dot_general | solution.py:22
  216.7 10.8 %fusion.2 = bf16[1536,1536]{1,0:T(8,128)(2,1)} fusion(f32[1536,1536]{1,0:T(8,128)S(1)} %fusion.16, bf16[768,1536]{0,1:T(8,128)(2,1)S(1)} %bitcast.308, bf16[768,768]{1,0:T(8,128)(2,1)} %bitcast.53, bf16[768,768]{1,0:T(8,128)(2,1)} %bitcast.52), kind=kOutput, calls=%fused_computation.8 | convolution fusion | flops 3671064576 | bytes 18874368 | tf_op jit(solution)/shard_map/dot_general | solution.py:22
  227.6 8.1 %fusion.14 = f32[768,1536]{1,0:T(8,128)} fusion(bf16[768,768]{1,0:T(8,128)(2,1)} %bitcast.53, bf16[768,768]{1,0:T(8,128)(2,1)} %bitcast.52, f32[1536,1536]{1,0:T(8,128)S(1)} %fusion.16), kind=kOutput, calls=%fused_computation.56 | convolution fusion | flops 3649830912 | bytes 16515072 | tf_op jit(solution)/shard_map/dot_general | solution.py:22
  235.6 6.7 %stack.268 = f32[1,768,4,384]{3,2,1,0:T(4,128)} reshape(f32[768,1536]{1,0:T(8,128)} %fusion.14) | data formatting | bytes 9437184 | tf_op jit(solution)/shard_map/stack | solution.py:369
  242.4 8.4 %fusion.77 = f32[1536,768]{1,0:T(8,128)} fusion(bf16[1536,1536]{1,0:T(8,128)(2,1)} %fusion.2, bf16[768,1536]{0,1:T(8,128)(2,1)S(1)} %bitcast.306), kind=kOutput, calls=%fused_computation.237 | convolution fusion | flops 3623878656 | bytes 11796480 | tf_op jit(solution)/shard_map/dot_general | solution.py:22
  250.8 9.1 %fusion.15 = f32[768,1536]{1,0:T(8,128)} fusion(bf16[1536,1536]{1,0:T(8,128)(2,1)} %fusion.2, bf16[768,768]{1,0:T(8,128)(2,1)} %collective-permute-done.17, bf16[768,768]{1,0:T(8,128)(2,1)} %multiply_convert_fusion.2), kind=kOutput, calls=%fused_computation.57 | convolution fusion | flops 3628597248 | bytes 11796480 | tf_op jit(solution)/shard_map/dot_general | solution.py:22
  259.8 6.2 %stack.267 = f32[1,768,4,384]{3,2,1,0:T(4,128)} reshape(f32[768,1536]{1,0:T(8,128)} %fusion.15) | data formatting | bytes 9437184 | tf_op jit(solution)/shard_map/stack | solution.py:369
  296.6 7.0 %collective-permute-done.46 = bf16[2,2,384,384]{3,2,1,0:T(8,128)(2,1)} collective-permute-done((bf16[2,2,384,384]{3,2,1,0:T(8,128)(2,1)}, bf16[2,2,384,384]{3,2,1,0:T(8,128)(2,1)}, u32[]{:S(2)}, u32[]{:S(2)}) %collective-permute-start.46) | collective-permute-done | bytes 1179680 | tf_op jit(solution)/shard_map/ppermute | solution.py:38
  313.2 9.3 %collective-permute-done.29 = bf16[192,3,256]{2,1,0:T(4,128)(2,1)S(1)} collective-permute-done((bf16[192,3,256]{2,1,0:T(4,128)(2,1)}, bf16[192,3,256]{2,1,0:T(4,128)(2,1)S(1)}, u32[]{:S(2)}, u32[]{:S(2)}) %collective-permute-start.29) | collective-permute-done | bytes 294944 | tf_op jit(solution)/shard_map/ppermute | solution.py:38
  340.7 44.4 %attend_back.1 = (bf16[5,3,64,1024]{3,2,1,0:T(8,128)(2,1)S(1)}, bf16[5,3,64,1024]{3,2,1,0:T(8,128)(2,1)}) custom-call(s32[1]{0:T(128)} %bitcast.1.c_ref, bf16[15,64,1024]{2,1,0:T(8,128)(2,1)S(1)} %copy-done.3, bf16[15,64,1024]{2,1,0:T(8,128)(2,1)S(1)} %copy-done.3, bf16[15,64,1024]{2,1,0:T(8,128)(2,1)S(1)} %copy-done.3, ...), custom_call_target="tpu_custom_call" | custom-call | flops 15099494400 | bytes 31457280 | tf_op jit(solution)/shard_map/attend_back/pallas_call | solution.py:198
  398.5 10.6 %reduce-scatter.12.cloned.1.call-done = bf16[192,96]{1,0:T(8,128)(2,1)} async-done(((bf16[768,96]{1,0:T(8,128)(2,1)}), bf16[192,96]{1,0:T(8,128)(2,1)}) %reduce-scatter.12.cloned.1.call-update) | async-done | bytes 36880
  426.1 8.1 %dot_general.50 = bf16[3,4,256,576]{2,1,0,3:T(4,128)(2,1)} reshape(bf16[3072,576]{0,1:T(8,128)(2,1)} %bitcast.291) | data formatting | bytes 7077888 | tf_op jit(solution)/shard_map/dot_general | solution.py:22
  434.2 6.0 %fusion.3 = f32[3,4,256,768]{3,2,1,0:T(8,128)S(1)} fusion(bf16[3,4,256,576]{2,1,0,3:T(4,128)(2,1)} %dot_general.50, bf16[768,576]{1,0:T(8,128)(2,1)S(1)} %copy-done.45), kind=kOutput, calls=%fused_computation.15 | convolution fusion | flops 2717908992 | bytes 13860864 | tf_op jit(solution)/shard_map/dot_general | solution.py:22
  452.7 16.9 %collective-permute-done.34 = bf16[2,3,128,768]{3,2,1,0:T(8,128)(2,1)} collective-permute-done((bf16[2,3,128,768]{3,2,1,0:T(8,128)(2,1)S(1)}, bf16[2,3,128,768]{3,2,1,0:T(8,128)(2,1)}, u32[]{:S(2)}, u32[]{:S(2)}) %collective-permute-start.34) | collective-permute-done | bytes 1179680 | tf_op jit(solution)/shard_map/ppermute | solution.py:38
  483.4 6.8 %all-reduce = (f32[192]{0:T(256)S(1)}, f32[192]{0:T(256)S(1)}) all-reduce(f32[192]{0:T(256)S(1)} %multiply_reduce_fusion.4, f32[192]{0:T(256)S(1)} %get-tuple-element.74), channel_id=1, replica_groups=mesh['dp'=4,'context'=2,'tensor'=4] {'tensor'}, use_global_device_ids=true, to_apply=%region_17.18 | all-reduce | flops 384 | bytes 3072 | tf_op jit(solution)/shard_map/psum | solution.py:382
  491.3 5.9 %collective-permute-done.33 = bf16[3,128,768]{2,1,0:T(8,128)(2,1)} collective-permute-done((bf16[3,128,768]{2,1,0:T(8,128)(2,1)}, bf16[3,128,768]{2,1,0:T(8,128)(2,1)}, u32[]{:S(2)}, u32[]{:S(2)}) %collective-permute-start.33) | collective-permute-done | bytes 589856 | tf_op jit(solution)/shard_map/ppermute | solution.py:38
  (397 shorter events, 221.6 us)
Async XLA Ops:
  7.2 152.7 %all-gather.4.cloned.1.call-start = ((), (), s32[]{:S(2)}) async-start(), calls=%async_computation.3 | async-start | bytes 1966080 | tf_op jit(solution)/shard_map/all_gather | solution.py:255
  18.0 170.2 %all-gather.6.cloned.1.call-start = ((), (), s32[]{:S(2)}) async-start(), calls=%async_computation.4 | async-start | bytes 5898240 | tf_op jit(solution)/shard_map/all_gather | solution.py:252
  18.9 40.5 %collective-permute-start.20 = (bf16[2,96,384]{2,1,0:T(8,128)(2,1)}, bf16[2,96,384]{2,1,0:T(8,128)(2,1)S(1)}, u32[]{:S(2)}, u32[]{:S(2)}) collective-permute-start(bf16[2,96,384]{2,1,0:T(8,128)(2,1)} %get-tuple-element.141), channel_id=1, source_target_pairs={{0,2},{1,3},{2,0},{3,1},{4,6},{5,7},{6,4},{7,5},{8,10},{9,11},{10,... | collective-permute-start | bytes 442376 | tf_op jit(solution)/shard_map/ppermute | solution.py:38
  20.5 39.0 %collective-permute-start.18 = (bf16[2,96,384]{2,1,0:T(8,128)(2,1)}, bf16[2,96,384]{2,1,0:T(8,128)(2,1)S(1)}, u32[]{:S(2)}, u32[]{:S(2)}) collective-permute-start(bf16[2,96,384]{2,1,0:T(8,128)(2,1)} %get-tuple-element.141), channel_id=1, source_target_pairs={{0,1},{1,0},{2,3},{3,2},{4,5},{5,4},{6,7},{7,6},{8,9},{9,8},{10,11... | collective-permute-start | bytes 442376 | tf_op jit(solution)/shard_map/ppermute | solution.py:38
  20.5 49.3 %collective-permute-start.21 = (bf16[2,96,384]{2,1,0:T(8,128)(2,1)}, bf16[2,96,384]{2,1,0:T(8,128)(2,1)S(1)}, u32[]{:S(2)}, u32[]{:S(2)}) collective-permute-start(bf16[2,96,384]{2,1,0:T(8,128)(2,1)} %get-tuple-element.142), channel_id=1, source_target_pairs={{0,2},{1,3},{2,0},{3,1},{4,6},{5,7},{6,4},{7,5},{8,10},{9,11},{10,... | collective-permute-start | bytes 442376 | tf_op jit(solution)/shard_map/ppermute | solution.py:38
  22.3 51.4 %collective-permute-start = (bf16[3,128,768]{2,1,0:T(8,128)(2,1)}, bf16[3,128,768]{2,1,0:T(8,128)(2,1)}, u32[]{:S(2)}, u32[]{:S(2)}) collective-permute-start(bf16[3,128,768]{2,1,0:T(8,128)(2,1)} %get-tuple-element.131), channel_id=1, source_target_pairs={{0,1},{1,0},{2,3},{3,2},{4,5},{5,4},{6,7},{7,6},{8,9},{9,8},{10,11... | collective-permute-start | bytes 1769480 | tf_op jit(solution)/shard_map/ppermute | solution.py:38
  23.0 50.9 %collective-permute-start.3 = (bf16[3,128,768]{2,1,0:T(8,128)(2,1)}, bf16[3,128,768]{2,1,0:T(8,128)(2,1)}, u32[]{:S(2)}, u32[]{:S(2)}) collective-permute-start(bf16[3,128,768]{2,1,0:T(8,128)(2,1)} %get-tuple-element.132), channel_id=1, source_target_pairs={{0,2},{1,3},{2,0},{3,1},{4,6},{5,7},{6,4},{7,5},{8,10},{9,11},{10,... | collective-permute-start | bytes 1769480 | tf_op jit(solution)/shard_map/ppermute | solution.py:38
  73.9 20.8 %collective-permute-start.5 = (bf16[3,128,768]{2,1,0:T(8,128)(2,1)}, bf16[3,128,768]{2,1,0:T(8,128)(2,1)}, u32[]{:S(2)}, u32[]{:S(2)}) collective-permute-start(bf16[3,128,768]{2,1,0:T(8,128)(2,1)} %collective-permute-done.3), channel_id=1, source_target_pairs={{0,1},{1,0},{2,3},{3,2},{4,5},{5,4},{6,7},{7,6},{8,9},{9,8},{10,11... | collective-permute-start | bytes 1769480 | tf_op jit(solution)/shard_map/ppermute | solution.py:38
  84.4 324.7 %reduce-scatter.12.cloned.1.call-start = ((), (), s32[]{:S(2)}) async-start(), calls=%async_computation.7 | async-start | bytes 245760
  184.2 32.6 %collective-permute-start.25 = (bf16[3,256,768]{2,1,0:T(8,128)(2,1)}, bf16[3,256,768]{2,1,0:T(8,128)(2,1)}, u32[]{:S(2)}, u32[]{:S(2)}) collective-permute-start(bf16[3,256,768]{2,1,0:T(8,128)(2,1)} %param.17), channel_id=1, source_target_pairs={{0,4},{4,0},{1,5},{5,1},{2,6},{6,2},{3,7},{7,3},{8,12},{12,8},{9,1... | collective-permute-start | bytes 3538952 | tf_op jit(solution)/shard_map/ppermute | solution.py:38
  276.1 27.5 %collective-permute-start.46 = (bf16[2,2,384,384]{3,2,1,0:T(8,128)(2,1)}, bf16[2,2,384,384]{3,2,1,0:T(8,128)(2,1)}, u32[]{:S(2)}, u32[]{:S(2)}) collective-permute-start(bf16[2,2,384,384]{3,2,1,0:T(8,128)(2,1)} %pad_maximum_fusion.18), channel_id=1, source_target_pairs={{0,2},{1,3},{2,0},{3,1},{4,6},{5,7},{6,4},{7,5},{8,10},{9,11},{10,... | collective-permute-start | bytes 3538952 | tf_op jit(solution)/shard_map/ppermute | solution.py:38
  277.7 30.4 %collective-permute-start.44 = (bf16[2,2,384,384]{3,2,1,0:T(8,128)(2,1)}, bf16[2,2,384,384]{3,2,1,0:T(8,128)(2,1)}, u32[]{:S(2)}, u32[]{:S(2)}) collective-permute-start(bf16[2,2,384,384]{3,2,1,0:T(8,128)(2,1)} %pad_maximum_fusion.17), channel_id=1, source_target_pairs={{0,1},{1,0},{2,3},{3,2},{4,5},{5,4},{6,7},{7,6},{8,9},{9,8},{10,11... | collective-permute-start | bytes 3538952 | tf_op jit(solution)/shard_map/ppermute | solution.py:38
  290.7 22.5 %collective-permute-start.27 = (bf16[192,3,256]{2,1,0:T(4,128)(2,1)}, bf16[192,3,256]{2,1,0:T(4,128)(2,1)S(1)}, u32[]{:S(2)}, u32[]{:S(2)}) collective-permute-start(bf16[192,3,256]{2,1,0:T(4,128)(2,1)} %squeeze.94), channel_id=1, source_target_pairs={{0,1},{1,0},{2,3},{3,2},{4,5},{5,4},{6,7},{7,6},{8,9},{9,8},{10,11... | collective-permute-start | bytes 884744 | tf_op jit(solution)/shard_map/ppermute | solution.py:38
  290.8 22.3 %collective-permute-start.28 = (bf16[192,3,256]{2,1,0:T(4,128)(2,1)}, bf16[192,3,256]{2,1,0:T(4,128)(2,1)S(1)}, u32[]{:S(2)}, u32[]{:S(2)}) collective-permute-start(bf16[192,3,256]{2,1,0:T(4,128)(2,1)} %squeeze.95), channel_id=1, source_target_pairs={{0,2},{1,3},{2,0},{3,1},{4,6},{5,7},{6,4},{7,5},{8,10},{9,11},{10,... | collective-permute-start | bytes 884744 | tf_op jit(solution)/shard_map/ppermute | solution.py:38
  292.3 30.1 %collective-permute-start.29 = (bf16[192,3,256]{2,1,0:T(4,128)(2,1)}, bf16[192,3,256]{2,1,0:T(4,128)(2,1)S(1)}, u32[]{:S(2)}, u32[]{:S(2)}) collective-permute-start(bf16[192,3,256]{2,1,0:T(4,128)(2,1)} %squeeze.96), channel_id=1, source_target_pairs={{0,3},{1,2},{2,1},{3,0},{4,7},{5,6},{6,5},{7,4},{8,11},{9,10},{10,... | collective-permute-start | bytes 884744 | tf_op jit(solution)/shard_map/ppermute | solution.py:38
  303.5 30.9 %collective-permute-start.38 = (bf16[4,96,768]{2,1,0:T(8,128)(2,1)}, bf16[4,96,768]{2,1,0:T(8,128)(2,1)}, u32[]{:S(2)}, u32[]{:S(2)}) collective-permute-start(bf16[4,96,768]{2,1,0:T(8,128)(2,1)} %dynamic-slice_convert_fusion.1), channel_id=1, source_target_pairs={{0,4},{4,0},{1,5},{5,1},{2,6},{6,2},{3,7},{7,3},{8,12},{12,8},{9,1... | collective-permute-start | bytes 1769480 | tf_op jit(solution)/shard_map/ppermute | solution.py:38
  308.1 86.2 %collective-permute-start.47 = (bf16[2,384,384]{2,1,0:T(8,128)(2,1)}, bf16[2,384,384]{2,1,0:T(8,128)(2,1)}, u32[]{:S(2)}, u32[]{:S(2)}) collective-permute-start(bf16[2,384,384]{2,1,0:T(8,128)(2,1)} %fusion.20), channel_id=1, source_target_pairs={{0,1},{1,0},{2,3},{3,2},{4,5},{5,4},{6,7},{7,6},{8,9},{9,8},{10,11... | collective-permute-start | bytes 1769480 | tf_op jit(solution)/shard_map/ppermute | solution.py:38
  337.6 56.7 %collective-permute-start.45 = (bf16[2,384,384]{2,1,0:T(8,128)(2,1)S(1)}, bf16[2,384,384]{2,1,0:T(8,128)(2,1)S(1)}, u32[]{:S(2)}, u32[]{:S(2)}) collective-permute-start(bf16[2,384,384]{2,1,0:T(8,128)(2,1)S(1)} %fusion.25), channel_id=1, source_target_pairs={{0,2},{1,3},{2,0},{3,1},{4,6},{5,7},{6,4},{7,5},{8,10},{9,11},{10,... | collective-permute-start | bytes 1769480 | tf_op jit(solution)/shard_map/ppermute | solution.py:38
  385.1 27.8 %collective-permute-start.31 = (bf16[5,3,64,1024]{3,2,1,0:T(8,128)(2,1)}, bf16[5,3,64,1024]{3,2,1,0:T(8,128)(2,1)}, u32[]{:S(2)}, u32[]{:S(2)}) collective-permute-start(bf16[5,3,64,1024]{3,2,1,0:T(8,128)(2,1)} %get-tuple-element.19), channel_id=1, source_target_pairs={{0,4},{4,0},{1,5},{5,1},{2,6},{6,2},{3,7},{7,3},{8,12},{12,8},{9,1... | collective-permute-start | bytes 5898248 | tf_op jit(solution)/shard_map/ppermute | solution.py:38
  394.3 53.8 %reduce-scatter.8.cloned.1.call-start = ((), (), s32[]{:S(2)}) async-start(), calls=%async_computation.5 | async-start | bytes 1474560 | tf_op jit(solution)/shard_map/reduce_scatter | solution.py:353
  398.4 78.0 %reduce-scatter.10.cloned.1.call-start = ((), (), s32[]{:S(2)}) async-start(), calls=%async_computation.6 | async-start | bytes 737280
  410.0 40.0 %collective-permute-start.43 = (bf16[96,192]{1,0:T(8,128)(2,1)S(1)}, bf16[96,192]{1,0:T(8,128)(2,1)S(1)}, u32[]{:S(2)}, u32[]{:S(2)}) collective-permute-start(bf16[96,192]{1,0:T(8,128)(2,1)S(1)} %copy.118), channel_id=1, source_target_pairs={{0,4},{4,0},{1,5},{5,1},{2,6},{6,2},{3,7},{7,3},{8,12},{12,8},{9,1... | collective-permute-start | bytes 110600 | tf_op jit(solution)/shard_map/ppermute | solution.py:38
  442.5 27.2 %collective-permute-start.34 = (bf16[2,3,128,768]{3,2,1,0:T(8,128)(2,1)S(1)}, bf16[2,3,128,768]{3,2,1,0:T(8,128)(2,1)}, u32[]{:S(2)}, u32[]{:S(2)}) collective-permute-start(bf16[2,3,128,768]{3,2,1,0:T(8,128)(2,1)S(1)} %pad_maximum_fusion.16), channel_id=1, source_target_pairs={{0,2},{1,3},{2,0},{3,1},{4,6},{5,7},{6,4},{7,5},{8,10},{9,11},{10,... | collective-permute-start | bytes 3538952 | tf_op jit(solution)/shard_map/ppermute | solution.py:38
  445.6 27.8 %collective-permute-start.32 = (bf16[2,3,128,768]{3,2,1,0:T(8,128)(2,1)}, bf16[2,3,128,768]{3,2,1,0:T(8,128)(2,1)}, u32[]{:S(2)}, u32[]{:S(2)}) collective-permute-start(bf16[2,3,128,768]{3,2,1,0:T(8,128)(2,1)} %pad_maximum_fusion.15), channel_id=1, source_target_pairs={{0,1},{1,0},{2,3},{3,2},{4,5},{5,4},{6,7},{7,6},{8,9},{9,8},{10,11... | collective-permute-start | bytes 3538952 | tf_op jit(solution)/shard_map/ppermute | solution.py:38
  (96 other events, 1098.5 us)
Sparse Core Ops, SparseCore 0:
  18.2 53.4 all-gather.3
  84.5 100.7 all-gather.5
  394.4 14.6 reduce-scatter.11
  411.4 29.3 reduce-scatter.7
  448.2 17.2 reduce-scatter.9

commit v2 on v1

--- a/solution.py
+++ b/solution.py
@@ -61,6 +61,17 @@
         return mine + across(theirs.astype(low), "tensor", second).astype(full)
 
     return jnp.concatenate([reduce(one, 1, 2), reduce(two, 2, 1)], axis=axis)
+
+
+def gather_dp(array, axis):
+    n = lax.axis_size("dp")
+    if n != 4:
+        return lax.all_gather(array, "dp", axis=axis, tiled=True)
+    parts = jnp.stack([across(array, "dp", r) if r else array for r in range(n)])
+    d = lax.axis_index("dp")
+    return jnp.concatenate(
+        [lax.dynamic_index_in_dim(parts, d ^ p, 0, False) for p in range(n)], axis=axis
+    )
 
 
 UNITS = 5
@@ -224,9 +235,100 @@
 def gelu_and_slope(v):
     k0 = math.sqrt(2.0 / math.pi)
     square = v * v
-    th = jnp.tanh(k0 * v * (1.0 + 0.044715 * square))
-    slope = 0.5 * (1.0 + th) + 0.5 * v * (1.0 - th * th) * k0 * (1.0 + 3.0 * 0.044715 * square)
-    return 0.5 * v * (1.0 + th), slope
+    th = jnp.tanh(v * (k0 + (k0 * 0.044715) * square))
+    half = 0.5 + 0.5 * th
+    slope = half + (v * half) * ((1.0 - th) * (k0 + (3.0 * 0.044715 * k0) * square))
+    return v * half, slope
+
+
+def feed_kernel(
+    xm, xt, gm, gt, up_ref, down_ref, om, ot, bm, bt, dup, ddown,
+    x, g, x_t, g_t, up, down, act, gh, out, back, pre, ga,
+):
+    rows, width = xm.shape
+    n = up_ref.shape[2]
+    blocks = 2 * rows // QB
+
+    @pl.when(pl.program_id(0) == 0)
+    def _():
+        for i, (a, b) in enumerate(((xm, gm), (xt, gt))):
+            part = slice(i * rows, (i + 1) * rows)
+            x[part, :] = a[...]
+            g[part, :] = b[...]
+            x_t[:, part] = a[...].T
+            g_t[:, part] = b[...].T
+        out[...] = jnp.zeros_like(out)
+        back[...] = jnp.zeros_like(back)
+
+    for i in range(2):
+        up[:, i * n : (i + 1) * n] = up_ref[i]
+        down[:, i * n : (i + 1) * n] = down_ref[i]
+
+    def first(i):
+        part = slice(i * QB, (i + 1) * QB)
+        pre[i % 2] = nn(x[part, :], up[...])
+        ga[i % 2] = nn(g[part, :], down[...])
+
+    def second(i):
+        part = slice(i * QB, (i + 1) * QB)
+        a, slope = gelu_and_slope(pre[i % 2])
+        act[part, :] = a.astype(low)
+        gh[part, :] = (ga[i % 2] * slope).astype(low)
+
+    def third(i):
+        part = slice(i * QB, (i + 1) * QB)
+        out[part, :] += nt(act[part, :], down[...])
+        back[part, :] += nt(gh[part, :], up[...])
+
+    first(0)
+    for i in range(blocks):
+        if i + 1 < blocks:
+            first(i + 1)
+        second(i)
+        if i > 0:
+            third(i - 1)
+    third(blocks - 1)
+    for m in range(0, width, QB):
+        part = slice(m, m + QB)
+        u = nn(x_t[part, :], gh[...]).astype(low)
+        v = nn(g_t[part, :], act[...]).astype(low)
+        for i in range(2):
+            dup[i, part, :] = u[:, i * n : (i + 1) * n]
+            ddown[i, part, :] = v[:, i * n : (i + 1) * n]
+
+    @pl.when(pl.program_id(0) == pl.num_programs(0) - 1)
+    def _():
+        om[...] = out[:rows, :]
+        ot[...] = out[rows:, :].astype(low)
+        bm[...] = back[:rows, :]
+        bt[...] = back[rows:, :].astype(low)
+
+
+def feed(xm, xt, gm, gt, up, down):
+    rows, width = xm.shape
+    pieces, _, n = up.shape
+    whole = pl.BlockSpec((rows, width), lambda j: (0, 0))
+    weight = pl.BlockSpec((2, width, n), lambda j: (j, 0, 0))
+    shape = jax.ShapeDtypeStruct
+    return pl.pallas_call(
+        feed_kernel,
+        grid=(pieces // 2,),
+        in_specs=[whole] * 4 + [weight] * 2,
+        out_specs=[whole] * 4 + [weight] * 2,
+        out_shape=[shape((rows, width), kind) for kind in (full, low, full, low)]
+        + [shape(up.shape, low)] * 2,
+        scratch_shapes=[pltpu.VMEM((2 * rows, width), low)] * 2
+        + [pltpu.VMEM((width, 2 * rows), low)] * 2
+        + [pltpu.VMEM((width, 2 * n), low)] * 2
+        + [pltpu.VMEM((2 * rows, 2 * n), low)] * 2
+        + [pltpu.VMEM((2 * rows, width), full)] * 2
+        + [pltpu.VMEM((2, QB, 2 * n), full)] * 2,
+        compiler_params=pltpu.CompilerParams(vmem_limit_bytes=60 << 20),
+        cost_estimate=pl.CostEstimate(
+            flops=6 * 2 * 2 * rows * width * pieces * n, bytes_accessed=20 << 20, transcendentals=0
+        ),
+        name="feed",
+    )(xm, xt, gm, gt, up, down)
 
 
 def per_device(tokens, segments, w_qkv, w_out, w_in, w_back, gain_attn, gain_mlp, cotangent):
@@ -243,16 +345,16 @@
 
     blocks = gather_tensor(tokens, 1)
     cot_theirs = across(cotangent, "context", 1)
-    w_attn = lax.all_gather(w_qkv.reshape(shard, 3 * local), "dp", axis=0, tiled=True)
-    gains = lax.all_gather(jnp.stack([gain_attn, gain_mlp], axis=1), "dp", axis=0, tiled=True)
+    w_attn = gather_dp(w_qkv.reshape(shard, 3 * local), 0)
+    gains = gather_dp(jnp.stack([gain_attn, gain_mlp], axis=1), 0)
     gain_first, gain_second = gains[:, 0].astype(full), gains[:, 1].astype(full)
     up_own = lax.dynamic_slice_in_dim(w_in, c * hidden, hidden, 1)
     down_own = lax.dynamic_slice_in_dim(w_back, c * hidden, hidden, 0).T
     up_down = jnp.stack(gather_tensor(jnp.stack([up_own, down_own]), 1), axis=1)
-    up_down = lax.all_gather(up_down, "dp", axis=2, tiled=True)
+    up_down = gather_dp(up_down, 2)
     w_up, w_down = up_down[0], up_down[1]
     w_proj = jnp.stack(gather_tensor(w_out.T, 0), axis=0)
-    w_proj = lax.all_gather(w_proj, "dp", axis=1, tiled=True)
+    w_proj = gather_dp(w_proj, 1)
 
     lo = jnp.zeros((sequences, length), jnp.int32)
     for value in range(8):
@@ -309,23 +411,12 @@
     inv_two = inverse(middle)
     normed_two = (middle * inv_two * gain_second).astype(low)
 
-    both = jnp.concatenate([normed_two, across(normed_two, "context", 1)], axis=0)
     cot = cotangent.reshape(rows, width)
-    both_cot = jnp.concatenate([cot, cot_theirs.reshape(rows, width)], axis=0)
-    up = w_up.transpose(1, 0, 2).reshape(width, 4 * hidden)
-    down = w_down.transpose(1, 0, 2).reshape(width, 4 * hidden)
-    hidden_pre = nn(both, up)
-    active, slope = gelu_and_slope(hidden_pre)
-    active = active.astype(low)
-    grad_hidden = (nn(both_cot, down) * slope).astype(low)
-    branch = nt(active, down)
-    back = nt(grad_hidden, up)
-    crossed = across(back[rows:].astype(low), "context", 1).astype(full)
-    grad_norm_two = back[:rows] + crossed
-    crossed = across(branch[rows:].astype(low), "context", 1).astype(full)
-    result = (middle + branch[:rows] + crossed).astype(low)
-    grad_down = tn(both_cot, active)
-    grad_up = tn(both, grad_hidden)
+    branch, branch_sent, back, back_sent, grad_up, grad_down = feed(
+        normed_two, across(normed_two, "context", 1), cot, cot_theirs.reshape(rows, width), w_up, w_down
+    )
+    grad_norm_two = back + across(back_sent, "context", 1).astype(full)
+    result = (middle + branch + across(branch_sent, "context", 1).astype(full)).astype(low)
 
     def norm_back(r, gain, v, inv):
         rg = r * gain
@@ -366,8 +457,8 @@
         sent = lax.dynamic_slice_in_dim(array, (1 - c) * size, size, axis)
         return mine + across(sent.astype(low), "context", 1).astype(full)
 
-    up_down = jnp.stack([grad_up, grad_down]).reshape(2, width, 4, hidden)
-    up_down = scatter_tensor([up_down[:, :, r] for r in range(4)], 1)
+    up_down = [jnp.stack([grad_up[r], grad_down[r]]).astype(full) for r in range(4)]
+    up_down = scatter_tensor(up_down, 1)
     up_down = scatter_dp(up_down, 1)
     own_up = swap_halves(up_down[0], 1).astype(full)
     own_down = swap_halves(up_down[1].T, 0).astype(full)

time: 518 us -> 579 us (1.12)
  waiting for transfers between devices: 89.9 us -> 217 us
  matrix products: 67.2 us -> 20.7 us
  blocking collectives: 51.3 us -> 6.52 us
  local copies, waits for them, and re-layouts: 99.9 us -> 63.3 us
  Pallas kernels: 67 us -> 100 us
  starting transfers between devices: 55.7 us -> 80.4 us
    ppermute x50 -> x62, waiting for transfers between devices: 79.2 us -> 180 us  [across(): lax.ppermute(array, axis, [(i, i ^ by) for i in range(lax.axis_size(axis))])]
    dot_general x12 -> x6, matrix products: 67.2 us -> 20.7 us  [dot(): lax.dot_general(left, right, (dims, ((), ())), preferred_element_type=full)]
    all_gather x2 -> x0, blocking collectives: 44.5 us -> none  [the longest x1 34.5 us: per_device(): lax.all_gather(w_qkv.reshape(shard, 3 * local), 'dp', axis=0, tiled=True)]
    pallas_call x0 -> x1, Pallas kernels: none -> 33.1 us  [feed(): pl.pallas_call(feed_kernel, grid=(pieces // 2,), in_specs=[whole] * 4 + [...]
    unnamed x7 -> x5, waiting for transfers between devices: 10.7 us -> 37.1 us
    ppermute x50 -> x62, starting transfers between devices: 55 us -> 80.3 us  [across(): lax.ppermute(array, axis, [(i, i ^ by) for i in range(lax.axis_size(axis))])]
    unnamed x144 -> x125, local copies, waits for them, and re-layouts: 29.9 us -> 12.9 us
    another operation x8 -> x3, local copies, waits for them, and re-layouts: 14.5 us -> 1.49 us  [the longest x2 1.37 us: per_device(): gains = gather_dp(jnp.stack([gain_attn, gain_mlp], axis=1), 0)]
  transfers between devices with their start and end apart: 55 -> 65, of which waited for: 20 -> 23; matrix products, arithmetic and copies ran while one was open for 31% -> 24% of each run, Pallas kernels for 13% -> 12%
where the time goes in v2:
time: 579 us; the launch traced here: 573 us
  waiting for transfers between devices  217 us (37%)
  Pallas kernels  100 us (17%)
  starting transfers between devices  80.4 us (14%)
  other arithmetic  69.8 us (12%)
  local copies, waits for them, and re-layouts  63.3 us (11%)
  matrix products  20.7 us (4%)
  between operations  15.4 us (3%)
  blocking collectives  6.52 us (1%)
    ppermute x62, waiting for transfers between devices, across(): lax.ppermute(array, axis, [(i, i ^ by) for i in range(lax.axis_size(axis))])  180 us
    ppermute x62, starting transfers between devices, across(): lax.ppermute(array, axis, [(i, i ^ by) for i in range(lax.axis_size(axis))])  80.3 us
    pallas_call x1, Pallas kernels, attend_back(): pl.pallas_call(attend_back_kernel, grid_spec=pltpu.PrefetchScalarGridSpec...  44.3 us
    unnamed x5, waiting for transfers between devices  37.1 us
    pallas_call x1, Pallas kernels, feed(): pl.pallas_call(feed_kernel, grid=(pieces // 2,), in_specs=[whole] * 4 + [...  33.1 us
    pallas_call x1, Pallas kernels, attend(): pl.pallas_call(attend_kernel, grid_spec=pltpu.PrefetchScalarGridSpec(num_...  22.7 us
    dot_general x6, matrix products, dot(): lax.dot_general(left, right, (dims, ((), ())), preferred_element_type=full)  20.7 us
    unnamed x125, local copies, waits for them, and re-layouts  12.9 us
  transfers between devices with their start and end apart: 65, of which 23 were waited for; matrix products, arithmetic and copies ran while one was open for 24% of the time, Pallas kernels for 12%

profile of v2, /device:TPU:1, one launch (start us, length us, event | category | flops | bytes accessed | tf_op | source)
XLA Modules:
  0.0 573.4 jit_solution(18372726067514959454)
XLA Ops:
  21.3 9.3 %collective-permute-done.19 = bf16[96,192]{0,1:T(8,128)(2,1)S(1)} collective-permute-done((bf16[96,192]{0,1:T(8,128)(2,1)S(1)}, bf16[96,192]{0,1:T(8,128)(2,1)S(1)}, u32[]{:S(2)}, u32[]{:S(2)}) %collective-permute-start.19) | collective-permute-done | bytes 36896 | tf_op jit(solution)/shard_map/ppermute | solution.py:38
  38.6 12.2 %collective-permute-start = (bf16[192,576]{0,1:T(8,128)(2,1)S(1)}, bf16[192,576]{0,1:T(8,128)(2,1)S(1)}, u32[]{:S(2)}, u32[]{:S(2)}) collective-permute-start(bf16[192,576]{0,1:T(8,128)(2,1)S(1)} %bitcast.344), channel_id=1, source_target_pairs={{0,8},{8,0},{16,24},{24,16},{1,9},{9,1},{17,25},{25,17},{2,10},{10... | collective-permute-start | bytes 663560 | tf_op jit(solution)/shard_map/ppermute | solution.py:38
  50.8 6.1 %collective-permute-done.1 = bf16[192,576]{0,1:T(8,128)(2,1)S(1)} collective-permute-done((bf16[192,576]{0,1:T(8,128)(2,1)S(1)}, bf16[192,576]{0,1:T(8,128)(2,1)S(1)}, u32[]{:S(2)}, u32[]{:S(2)}) %collective-permute-start.1) | collective-permute-done | bytes 221216 | tf_op jit(solution)/shard_map/ppermute | solution.py:38
  72.6 9.1 %collective-permute-done.8 = bf16[3,128,768]{2,1,0:T(8,128)(2,1)S(1)} collective-permute-done((bf16[3,128,768]{2,1,0:T(8,128)(2,1)S(1)}, bf16[3,128,768]{2,1,0:T(8,128)(2,1)S(1)}, u32[]{:S(2)}, u32[]{:S(2)}) %collective-permute-start.8) | collective-permute-done | bytes 589856 | tf_op jit(solution)/shard_map/ppermute | solution.py:38
  89.7 5.6 convolution_convert_fusion
  96.2 6.0 %collective-permute-start.12 = (bf16[15,64,1024]{2,1,0:T(8,128)(2,1)S(1)}, bf16[15,64,1024]{2,1,0:T(8,128)(2,1)S(1)}, u32[]{:S(2)}, u32[]{:S(2)}) collective-permute-start(bf16[15,64,1024]{2,1,0:T(8,128)(2,1)S(1)} %pad_maximum_fusion.5), channel_id=1, source_target_pairs={{0,4},{4,0},{1,5},{5,1},{2,6},{6,2},{3,7},{7,3},{8,12},{12,8},{9,1... | collective-permute-start | bytes 5898248 | tf_op jit(solution)/shard_map/ppermute | solution.py:38
  113.3 10.9 %collective-permute-done.24 = bf16[4,192,192]{1,2,0:T(8,128)(2,1)S(1)} collective-permute-done((bf16[4,192,192]{1,2,0:T(8,128)(2,1)S(1)}, bf16[4,192,192]{1,2,0:T(8,128)(2,1)S(1)}, u32[]{:S(2)}, u32[]{:S(2)}) %collective-permute-start.24) | collective-permute-done | bytes 294944 | tf_op jit(solution)/shard_map/ppermute | solution.py:38
  124.2 9.7 %collective-permute-done.23 = bf16[4,192,192]{1,2,0:T(8,128)(2,1)S(1)} collective-permute-done((bf16[4,192,192]{1,2,0:T(8,128)(2,1)S(1)}, bf16[4,192,192]{1,2,0:T(8,128)(2,1)S(1)}, u32[]{:S(2)}, u32[]{:S(2)}) %collective-permute-start.23) | collective-permute-done | bytes 294944 | tf_op jit(solution)/shard_map/ppermute | solution.py:38
  140.8 22.7 %attend.1 = (bf16[5,64,1024]{2,1,0:T(8,128)(2,1)S(1)}, bf16[5,64,1024]{2,1,0:T(8,128)(2,1)S(1)}, f32[5,1,2048]{2,1,0:T(1,128)S(1)}, f32[5,64,2048]{2,1,0:T(8,128)S(1)}) custom-call(s32[1]{0:T(128)} %bitcast.1.c_ref, bf16[15,64,1024]{2,1,0:T(8,128)(2,1)S(1)} %pad_maximum_fusion.4.qm.km.vm, bf16[15,64,1024]{2,1,0:T(8,128)(2,1)S(1)} %pad_maximum_fusion.4.qm.km.vm, ...), custom_call_target="tpu_custom_call" | custom-call | flops 6039797760 | bytes 20971520 | tf_op jit(solution)/shard_map/attend/pallas_call | solution.py:127
  165.3 51.3 %collective-permute-done.35 = bf16[2,4,192,384]{3,2,0,1:T(8,128)(2,1)S(1)} collective-permute-done((bf16[2,4,192,384]{3,2,0,1:T(8,128)(2,1)S(1)}, bf16[2,4,192,384]{3,2,0,1:T(8,128)(2,1)S(1)}, u32[]{:S(2)}, u32[]{:S(2)}) %collective-permute-start.35) | collective-permute-done | bytes 1179680 | tf_op jit(solution)/shard_map/ppermute | solution.py:38
  226.5 8.2 %collective-permute-done.16 = bf16[3,192,256]{2,0,1:T(4,128)(2,1)S(1)} collective-permute-done((bf16[3,192,256]{2,0,1:T(4,128)(2,1)S(1)}, bf16[3,192,256]{2,0,1:T(4,128)(2,1)S(1)}, u32[]{:S(2)}, u32[]{:S(2)}) %collective-permute-start.16) | collective-permute-done | bytes 294944 | tf_op jit(solution)/shard_map/ppermute | solution.py:38
  234.6 9.3 %collective-permute-done.15 = bf16[3,192,256]{2,0,1:T(4,128)(2,1)S(1)} collective-permute-done((bf16[3,192,256]{2,0,1:T(4,128)(2,1)S(1)}, bf16[3,192,256]{2,0,1:T(4,128)(2,1)S(1)}, u32[]{:S(2)}, u32[]{:S(2)}) %collective-permute-start.15) | collective-permute-done | bytes 294944 | tf_op jit(solution)/shard_map/ppermute | solution.py:38
  256.7 33.1 %feed.1 = (f32[768,768]{1,0:T(8,128)}, bf16[768,768]{1,0:T(8,128)(2,1)}, f32[768,768]{1,0:T(8,128)}, bf16[768,768]{1,0:T(8,128)(2,1)}, bf16[4,768,384]{2,1,0:T(8,128)(2,1)}, /*index=5*/bf16[4,768,384]{2,1,0:T(8,128)(2,1)}) custom-call(bf16[768,768]{1,0:T(8,128)(2,1)} %multiply_convert_fusion.1.xm, bf16[768,768]{1,0:T(8,128)(2,1)} %collective-permute-done.26.xt, ...), custom_call_target="tpu_custom_call" | custom-call | flops 21743271936 | bytes 20971520 | tf_op jit(solution)/shard_map/feed/pallas_call | solution.py:313
  319.9 4.1 collective-permute-done.58
  326.8 6.9 %collective-permute-done.39 = bf16[192,3,256]{2,1,0:T(4,128)(2,1)} collective-permute-done((bf16[192,3,256]{2,1,0:T(4,128)(2,1)}, bf16[192,3,256]{2,1,0:T(4,128)(2,1)}, u32[]{:S(2)}, u32[]{:S(2)}) %collective-permute-start.39) | collective-permute-done | bytes 294944 | tf_op jit(solution)/shard_map/ppermute | solution.py:38
  333.7 9.3 %collective-permute-done.41 = bf16[192,3,256]{2,1,0:T(4,128)(2,1)} collective-permute-done((bf16[192,3,256]{2,1,0:T(4,128)(2,1)}, bf16[192,3,256]{2,1,0:T(4,128)(2,1)}, u32[]{:S(2)}, u32[]{:S(2)}) %collective-permute-start.41) | collective-permute-done | bytes 294944 | tf_op jit(solution)/shard_map/ppermute | solution.py:38
  360.8 44.3 %attend_back.1 = (bf16[5,3,64,1024]{3,2,1,0:T(8,128)(2,1)S(1)}, bf16[5,3,64,1024]{3,2,1,0:T(8,128)(2,1)}) custom-call(s32[1]{0:T(128)} %bitcast.1.c_ref, bf16[15,64,1024]{2,1,0:T(8,128)(2,1)S(1)} %copy-done.3, bf16[15,64,1024]{2,1,0:T(8,128)(2,1)S(1)} %copy-done.3, bf16[15,64,1024]{2,1,0:T(8,128)(2,1)S(1)} %copy-done.3, ...), custom_call_target="tpu_custom_call" | custom-call | flops 15099494400 | bytes 31457280 | tf_op jit(solution)/shard_map/attend_back/pallas_call | solution.py:209
  415.9 11.0 %collective-permute-done.52 = bf16[48,768]{1,0:T(8,128)(2,1)S(1)} collective-permute-done((bf16[48,768]{1,0:T(8,128)(2,1)S(1)}, bf16[48,768]{1,0:T(8,128)(2,1)S(1)}, u32[]{:S(2)}, u32[]{:S(2)}) %collective-permute-start.52) | collective-permute-done | bytes 73760 | tf_op jit(solution)/shard_map/ppermute | solution.py:38
  432.1 37.1 %reduce-scatter.12.cloned.1.call-done = bf16[192,96]{1,0:T(8,128)(2,1)} async-done(((bf16[768,96]{1,0:T(8,128)(2,1)}), bf16[192,96]{1,0:T(8,128)(2,1)}) %reduce-scatter.12.cloned.1.call-update) | async-done | bytes 36880
  486.3 7.8 %dot_general.28 = bf16[3,4,256,576]{2,1,0,3:T(4,128)(2,1)} reshape(bf16[3072,576]{0,1:T(8,128)(2,1)} %bitcast.317) | data formatting | bytes 7077888 | tf_op jit(solution)/shard_map/dot_general | solution.py:22
  494.2 6.0 %fusion.2 = f32[3,4,256,768]{3,2,1,0:T(8,128)S(1)} fusion(bf16[3,4,256,576]{2,1,0,3:T(4,128)(2,1)} %dot_general.28, bf16[192,576]{0,1:T(8,128)(2,1)S(1)} %copy-done.48, bf16[192,576]{0,1:T(8,128)(2,1)S(1)} %copy-done.50, bf16[192,576]{0,1:T(8,128)(2,1)S(1)} %copy-done.52, bf16[192,576]{0,1:T(8,128)(2,1)S(1)} %copy-done.46), kind=kOutput, calls=%fused_computation.11 | convolution fusion | flops 2721447936 | bytes 13860864 | tf_op jit(solution)/shard_map/dot_general | solution.py:22
  513.6 17.3 %collective-permute-done.46 = bf16[2,3,128,768]{3,2,1,0:T(8,128)(2,1)} collective-permute-done((bf16[2,3,128,768]{3,2,1,0:T(8,128)(2,1)S(1)}, bf16[2,3,128,768]{3,2,1,0:T(8,128)(2,1)}, u32[]{:S(2)}, u32[]{:S(2)}) %collective-permute-start.46) | collective-permute-done | bytes 1179680 | tf_op jit(solution)/shard_map/ppermute | solution.py:38
  544.5 6.5 %all-reduce = (f32[192]{0:T(256)S(1)}, f32[192]{0:T(256)S(1)}) all-reduce(f32[192]{0:T(256)S(1)} %multiply_reduce_fusion.4, f32[192]{0:T(256)S(1)} %get-tuple-element.78), channel_id=1, replica_groups=mesh['dp'=4,'context'=2,'tensor'=4] {'tensor'}, use_global_device_ids=true, to_apply=%region_17.18 | all-reduce | flops 384 | bytes 3072 | tf_op jit(solution)/shard_map/psum | solution.py:473
  552.2 6.1 %collective-permute-done.45 = bf16[3,128,768]{2,1,0:T(8,128)(2,1)} collective-permute-done((bf16[3,128,768]{2,1,0:T(8,128)(2,1)}, bf16[3,128,768]{2,1,0:T(8,128)(2,1)}, u32[]{:S(2)}, u32[]{:S(2)}) %collective-permute-start.45) | collective-permute-done | bytes 589856 | tf_op jit(solution)/shard_map/ppermute | solution.py:38
  (393 shorter events, 207.9 us)
Async XLA Ops:
  7.2 462.0 %reduce-scatter.12.cloned.1.call-start = ((), (), s32[]{:S(2)}) async-start(), calls=%async_computation.5 | async-start | bytes 245760
  15.3 43.9 %collective-permute-start.3 = (bf16[3,128,768]{2,1,0:T(8,128)(2,1)}, bf16[3,128,768]{2,1,0:T(8,128)(2,1)S(1)}, u32[]{:S(2)}, u32[]{:S(2)}) collective-permute-start(bf16[3,128,768]{2,1,0:T(8,128)(2,1)} %get-tuple-element.154), channel_id=1, source_target_pairs={{0,1},{1,0},{2,3},{3,2},{4,5},{5,4},{6,7},{7,6},{8,9},{9,8},{10,11... | collective-permute-start | bytes 1769480 | tf_op jit(solution)/shard_map/ppermute | solution.py:38
  16.5 44.0 %collective-permute-start.6 = (bf16[3,128,768]{2,1,0:T(8,128)(2,1)S(1)}, bf16[3,128,768]{2,1,0:T(8,128)(2,1)S(1)}, u32[]{:S(2)}, u32[]{:S(2)}) collective-permute-start(bf16[3,128,768]{2,1,0:T(8,128)(2,1)S(1)} %get-tuple-element.155), channel_id=1, source_target_pairs={{0,2},{1,3},{2,0},{3,1},{4,6},{5,7},{6,4},{7,5},{8,10},{9,11},{10,... | collective-permute-start | bytes 1769480 | tf_op jit(solution)/shard_map/ppermute | solution.py:38
  34.2 31.2 %collective-permute-start.5 = (bf16[3,128,768]{2,1,0:T(8,128)(2,1)}, bf16[3,128,768]{2,1,0:T(8,128)(2,1)S(1)}, u32[]{:S(2)}, u32[]{:S(2)}) collective-permute-start(bf16[3,128,768]{2,1,0:T(8,128)(2,1)} %get-tuple-element.154), channel_id=1, source_target_pairs={{0,2},{1,3},{2,0},{3,1},{4,6},{5,7},{6,4},{7,5},{8,10},{9,11},{10,... | collective-permute-start | bytes 1769480 | tf_op jit(solution)/shard_map/ppermute | solution.py:38
  62.3 42.4 %collective-permute-start.30 = (bf16[2,96,384]{2,1,0:T(8,128)(2,1)}, bf16[2,96,384]{2,1,0:T(8,128)(2,1)}, u32[]{:S(2)}, u32[]{:S(2)}) collective-permute-start(bf16[2,96,384]{2,1,0:T(8,128)(2,1)} %get-tuple-element.166), channel_id=1, source_target_pairs={{0,2},{1,3},{2,0},{3,1},{4,6},{5,7},{6,4},{7,5},{8,10},{9,11},{10,... | collective-permute-start | bytes 442376 | tf_op jit(solution)/shard_map/ppermute | solution.py:38
  65.4 37.7 %collective-permute-start.28 = (bf16[2,96,384]{2,1,0:T(8,128)(2,1)}, bf16[2,96,384]{2,1,0:T(8,128)(2,1)}, u32[]{:S(2)}, u32[]{:S(2)}) collective-permute-start(bf16[2,96,384]{2,1,0:T(8,128)(2,1)} %get-tuple-element.166), channel_id=1, source_target_pairs={{0,1},{1,0},{2,3},{3,2},{4,5},{5,4},{6,7},{7,6},{8,9},{9,8},{10,11... | collective-permute-start | bytes 442376 | tf_op jit(solution)/shard_map/ppermute | solution.py:38
  69.1 35.7 %collective-permute-start.31 = (bf16[2,96,384]{2,1,0:T(8,128)(2,1)}, bf16[2,96,384]{2,1,0:T(8,128)(2,1)S(1)}, u32[]{:S(2)}, u32[]{:S(2)}) collective-permute-start(bf16[2,96,384]{2,1,0:T(8,128)(2,1)} %get-tuple-element.167), channel_id=1, source_target_pairs={{0,2},{1,3},{2,0},{3,1},{4,6},{5,7},{6,4},{7,5},{8,10},{9,11},{10,... | collective-permute-start | bytes 442376 | tf_op jit(solution)/shard_map/ppermute | solution.py:38
  96.2 44.6 %collective-permute-start.12 = (bf16[15,64,1024]{2,1,0:T(8,128)(2,1)S(1)}, bf16[15,64,1024]{2,1,0:T(8,128)(2,1)S(1)}, u32[]{:S(2)}, u32[]{:S(2)}) collective-permute-start(bf16[15,64,1024]{2,1,0:T(8,128)(2,1)S(1)} %pad_maximum_fusion.5), channel_id=1, source_target_pairs={{0,4},{4,0},{1,5},{5,1},{2,6},{6,2},{3,7},{7,3},{8,12},{12,8},{9,1... | collective-permute-start | bytes 5898248 | tf_op jit(solution)/shard_map/ppermute | solution.py:38
  111.5 145.1 %collective-permute-start.27 = (bf16[3,256,768]{2,1,0:T(8,128)(2,1)S(1)}, bf16[3,256,768]{2,1,0:T(8,128)(2,1)}, u32[]{:S(2)}, u32[]{:S(2)}) collective-permute-start(bf16[3,256,768]{2,1,0:T(8,128)(2,1)S(1)} %copy-done.34), channel_id=1, source_target_pairs={{0,4},{4,0},{1,5},{5,1},{2,6},{6,2},{3,7},{7,3},{8,12},{12,8},{9,1... | collective-permute-start | bytes 3538952 | tf_op jit(solution)/shard_map/ppermute | solution.py:38
  124.2 92.4 %collective-permute-start.35 = (bf16[2,4,192,384]{3,2,0,1:T(8,128)(2,1)S(1)}, bf16[2,4,192,384]{3,2,0,1:T(8,128)(2,1)S(1)}, u32[]{:S(2)}, u32[]{:S(2)}) collective-permute-start(bf16[2,4,192,384]{3,2,0,1:T(8,128)(2,1)S(1)} %get-tuple-element.147), channel_id=1, source_target_pairs={{0,16},{8,24},{16,0},{24,8},{1,17},{9,25},{17,1},{25,9},{2,18},{10... | collective-permute-start | bytes 3538952 | tf_op jit(solution)/shard_map/ppermute | solution.py:38
  134.0 82.6 %collective-permute-start.34 = (bf16[2,4,192,384]{3,2,0,1:T(8,128)(2,1)S(1)}, bf16[2,4,192,384]{3,2,0,1:T(8,128)(2,1)S(1)}, u32[]{:S(2)}, u32[]{:S(2)}) collective-permute-start(bf16[2,4,192,384]{3,2,0,1:T(8,128)(2,1)S(1)} %get-tuple-element.147), channel_id=1, source_target_pairs={{0,8},{8,0},{16,24},{24,16},{1,9},{9,1},{17,25},{25,17},{2,10},{10... | collective-permute-start | bytes 3538952 | tf_op jit(solution)/shard_map/ppermute | solution.py:38
  134.0 82.6 %collective-permute-start.36 = (bf16[2,4,192,384]{3,2,0,1:T(8,128)(2,1)S(1)}, bf16[2,4,192,384]{3,2,0,1:T(8,128)(2,1)S(1)}, u32[]{:S(2)}, u32[]{:S(2)}) collective-permute-start(bf16[2,4,192,384]{3,2,0,1:T(8,128)(2,1)S(1)} %get-tuple-element.147), channel_id=1, source_target_pairs={{0,24},{8,16},{16,8},{24,0},{1,25},{9,17},{17,9},{25,1},{2,26},{10... | collective-permute-start | bytes 3538952 | tf_op jit(solution)/shard_map/ppermute | solution.py:38
  163.5 54.7 %collective-permute-start.13 = (bf16[5,64,1024]{2,1,0:T(8,128)(2,1)S(1)}, bf16[5,64,1024]{2,1,0:T(8,128)(2,1)S(1)}, u32[]{:S(2)}, u32[]{:S(2)}) collective-permute-start(bf16[5,64,1024]{2,1,0:T(8,128)(2,1)S(1)} %get-tuple-element.21), channel_id=1, source_target_pairs={{0,4},{4,0},{1,5},{5,1},{2,6},{6,2},{3,7},{7,3},{8,12},{12,8},{9,1... | collective-permute-start | bytes 1966088 | tf_op jit(solution)/shard_map/ppermute | solution.py:38
  296.2 27.9 %collective-permute-start.58 = (bf16[2,2,384,384]{3,2,1,0:T(8,128)(2,1)}, bf16[2,2,384,384]{3,2,1,0:T(8,128)(2,1)}, u32[]{:S(2)}, u32[]{:S(2)}) collective-permute-start(bf16[2,2,384,384]{3,2,1,0:T(8,128)(2,1)} %pad_maximum_fusion.17), channel_id=1, source_target_pairs={{0,2},{1,3},{2,0},{3,1},{4,6},{5,7},{6,4},{7,5},{8,10},{9,11},{10,... | collective-permute-start | bytes 3538952 | tf_op jit(solution)/shard_map/ppermute | solution.py:38
  297.8 58.1 %collective-permute-start.56 = (bf16[2,2,384,384]{3,2,1,0:T(8,128)(2,1)}, bf16[2,2,384,384]{3,2,1,0:T(8,128)(2,1)}, u32[]{:S(2)}, u32[]{:S(2)}) collective-permute-start(bf16[2,2,384,384]{3,2,1,0:T(8,128)(2,1)} %pad_maximum_fusion.16), channel_id=1, source_target_pairs={{0,1},{1,0},{2,3},{3,2},{4,5},{5,4},{6,7},{7,6},{8,9},{9,8},{10,11... | collective-permute-start | bytes 3538952 | tf_op jit(solution)/shard_map/ppermute | solution.py:38
  311.9 31.1 %collective-permute-start.41 = (bf16[192,3,256]{2,1,0:T(4,128)(2,1)}, bf16[192,3,256]{2,1,0:T(4,128)(2,1)}, u32[]{:S(2)}, u32[]{:S(2)}) collective-permute-start(bf16[192,3,256]{2,1,0:T(4,128)(2,1)} %squeeze.152), channel_id=1, source_target_pairs={{0,3},{1,2},{2,1},{3,0},{4,7},{5,6},{6,5},{7,4},{8,11},{9,10},{10,... | collective-permute-start | bytes 884744 | tf_op jit(solution)/shard_map/ppermute | solution.py:38
  324.1 33.5 %collective-permute-start.50 = (bf16[4,96,768]{2,1,0:T(8,128)(2,1)}, bf16[4,96,768]{2,1,0:T(8,128)(2,1)}, u32[]{:S(2)}, u32[]{:S(2)}) collective-permute-start(bf16[4,96,768]{2,1,0:T(8,128)(2,1)} %dynamic-slice_convert_fusion.1), channel_id=1, source_target_pairs={{0,4},{4,0},{1,5},{5,1},{2,6},{6,2},{3,7},{7,3},{8,12},{12,8},{9,1... | collective-permute-start | bytes 1769480 | tf_op jit(solution)/shard_map/ppermute | solution.py:38
  355.4 72.5 %collective-permute-start.59 = (bf16[2,384,384]{2,1,0:T(8,128)(2,1)}, bf16[2,384,384]{2,1,0:T(8,128)(2,1)}, u32[]{:S(2)}, u32[]{:S(2)}) collective-permute-start(bf16[2,384,384]{2,1,0:T(8,128)(2,1)} %fusion.12), channel_id=1, source_target_pairs={{0,1},{1,0},{2,3},{3,2},{4,5},{5,4},{6,7},{7,6},{8,9},{9,8},{10,11... | collective-permute-start | bytes 1769480 | tf_op jit(solution)/shard_map/ppermute | solution.py:38
  405.1 67.9 %collective-permute-start.43 = (bf16[5,3,64,1024]{3,2,1,0:T(8,128)(2,1)}, bf16[5,3,64,1024]{3,2,1,0:T(8,128)(2,1)}, u32[]{:S(2)}, u32[]{:S(2)}) collective-permute-start(bf16[5,3,64,1024]{3,2,1,0:T(8,128)(2,1)} %get-tuple-element.29), channel_id=1, source_target_pairs={{0,4},{4,0},{1,5},{5,1},{2,6},{6,2},{3,7},{7,3},{8,12},{12,8},{9,1... | collective-permute-start | bytes 5898248 | tf_op jit(solution)/shard_map/ppermute | solution.py:38
  427.8 80.8 %reduce-scatter.8.cloned.1.call-start = ((), (), s32[]{:S(2)}) async-start(), calls=%async_computation.3 | async-start | bytes 1474560 | tf_op jit(solution)/shard_map/reduce_scatter | solution.py:444
  431.9 105.6 %reduce-scatter.10.cloned.1.call-start = ((), (), s32[]{:S(2)}) async-start(), calls=%async_computation.4 | async-start | bytes 737280
  470.1 40.8 %collective-permute-start.55 = (bf16[96,192]{1,0:T(8,128)(2,1)S(1)}, bf16[96,192]{1,0:T(8,128)(2,1)S(1)}, u32[]{:S(2)}, u32[]{:S(2)}) collective-permute-start(bf16[96,192]{1,0:T(8,128)(2,1)S(1)} %copy.81), channel_id=1, source_target_pairs={{0,4},{4,0},{1,5},{5,1},{2,6},{6,2},{3,7},{7,3},{8,12},{12,8},{9,1... | collective-permute-start | bytes 110600 | tf_op jit(solution)/shard_map/ppermute | solution.py:38
  503.7 27.1 %collective-permute-start.46 = (bf16[2,3,128,768]{3,2,1,0:T(8,128)(2,1)S(1)}, bf16[2,3,128,768]{3,2,1,0:T(8,128)(2,1)}, u32[]{:S(2)}, u32[]{:S(2)}) collective-permute-start(bf16[2,3,128,768]{3,2,1,0:T(8,128)(2,1)S(1)} %pad_maximum_fusion.15), channel_id=1, source_target_pairs={{0,2},{1,3},{2,0},{3,1},{4,6},{5,7},{6,4},{7,5},{8,10},{9,11},{10,... | collective-permute-start | bytes 3538952 | tf_op jit(solution)/shard_map/ppermute | solution.py:38
  506.1 28.5 %collective-permute-start.44 = (bf16[2,3,128,768]{3,2,1,0:T(8,128)(2,1)}, bf16[2,3,128,768]{3,2,1,0:T(8,128)(2,1)}, u32[]{:S(2)}, u32[]{:S(2)}) collective-permute-start(bf16[2,3,128,768]{3,2,1,0:T(8,128)(2,1)} %pad_maximum_fusion.14), channel_id=1, source_target_pairs={{0,1},{1,0},{2,3},{3,2},{4,5},{5,4},{6,7},{7,6},{8,9},{9,8},{10,11... | collective-permute-start | bytes 3538952 | tf_op jit(solution)/shard_map/ppermute | solution.py:38
  (99 other events, 1158.8 us)
Sparse Core Ops, SparseCore 0:
  428.0 41.1 reduce-scatter.11
  471.6 29.4 reduce-scatter.7
  508.7 16.9 reduce-scatter.9

commit v3 on v2

--- a/solution.py
+++ b/solution.py
@@ -75,18 +75,54 @@
 
 
 UNITS = 5
+PEERS = [(dc, r) for dc in range(2) for r in range(4)]
+
+
+def place():
+    return lax.axis_index("context"), lax.axis_index("tensor")
+
+
+def at_peer(c, t, dc, r):
+    return {"context": c ^ dc, "tensor": t ^ r}
+
+
+def greet(c, t):
+    barrier = pltpu.get_barrier_semaphore()
+    for dc, r in PEERS[1:]:
+        pl.semaphore_signal(barrier, inc=1, device_id=at_peer(c, t, dc, r))
+
+
+def greeted():
+    pl.semaphore_wait(pltpu.get_barrier_semaphore(), len(PEERS) - 1)
+
+
+def unit_place(u, c):
+    return jnp.where(u < 3, u, c + u - 3), jnp.where(u < 3, 2 * c, 1)
+
+
+def sends(u, c):
+    return (u != 3) | (c == 0)
 
 
 def unit_block(part):
-    return lambda u, c: (jnp.where(u < 3, part * 3 + u, 9 + part * 2 + (u - 3)), 0, 0)
-
-
-def attend_kernel(c_ref, qm, km, vm, qt, kt, vt, lo_ref, om, ot, lse_ref, of_ref, qs, ks, vs, ss):
-    c = c_ref[0]
+    return lambda u: (jnp.where(u < 3, part * 3 + u, 9 + part * 2 + (u - 3)), 0, 0)
+
+
+def attend_kernel(
+    qm, km, vm, qt, kt, vt, lo_ref, att, lse_ref, of_ref, qs, ks, vs, ss, obuf, ssem, rsem, lsem
+):
+    u = pl.program_id(0)
+    c, t = place()
     length = lo_ref.shape[2]
     half = length // 2
-    for place, q, k, v in ((c, qm, km, vm), (1 - c, qt, kt, vt)):
-        off = pl.multiple_of(place * half, half)
+    own = half // 4
+
+    @pl.when(u == 0)
+    def _():
+        greet(c, t)
+
+    for core, q, k, v in ((c, qm, km, vm), (1 - c, qt, kt, vt)):
+        off = pl.multiple_of(core * half, half)
         qs[:, pl.ds(off, half)] = q[0] * low(0.125)
         vs[:, pl.ds(off, half)] = v[0]
         ks[pl.ds(off, half), :] = k[0].T
@@ -114,63 +150,147 @@
             acc += nn(vs[:, at : at + CHUNK], p.astype(low))
         total = jnp.sum(total, axis=0, keepdims=True)
         lse_ref[0, :, start:stop] = most + jnp.log(total)
-        of_ref[0, :, start:stop] = acc * (1.0 / total)
-    om[0] = of_ref[0, :, pl.ds(pl.multiple_of(c * half, half), half)].astype(low)
-    ot[0] = of_ref[0, :, pl.ds(pl.multiple_of((1 - c) * half, half), half)].astype(low)
-
-
-def attend(c, mine, theirs, lo):
+        o = acc * (1.0 / total)
+        of_ref[0, :, start:stop] = o
+        obuf[u, :, start:stop] = o.astype(low)
+
+    @pl.when(u == 0)
+    def _():
+        greeted()
+
+    def move(unit, i, source_core):
+        dc, r = PEERS[i]
+        h, seq = unit_place(unit, source_core)
+        dest = pl.multiple_of(((c ^ dc) * 4 + (t ^ r)) * own, own)
+        src = obuf.at[unit, :, pl.ds(dest, own)]
+        dst = att.at[
+            pl.ds(pl.multiple_of((t * 3 + h) * HD, HD), HD), pl.ds(pl.multiple_of(seq * own, own), own)
+        ]
+        if i == 0:
+            return pltpu.make_async_copy(src, dst, lsem.at[unit])
+        return pltpu.make_async_remote_copy(
+            src, dst, ssem.at[i - 1, unit], rsem.at[i - 1, unit], device_id=at_peer(c, t, dc, r)
+        )
+
+    @pl.when(sends(u, c))
+    def _():
+        for i in range(1, len(PEERS)):
+            move(u, i, c).start()
+        move(u, 0, c).start()
+
+    @pl.when(u == pl.num_programs(0) - 1)
+    def _():
+        for unit in range(UNITS):
+            for i, (dc, r) in enumerate(PEERS):
+
+                @pl.when(sends(unit, c))
+                def _():
+                    if i:
+                        move(unit, i, c).wait_send()
+                    else:
+                        move(unit, i, c).wait()
+
+                if i:
+
+                    @pl.when(sends(unit, c ^ dc))
+                    def _():
+                        move(unit, i, c ^ dc).wait_recv()
+
+
+def attend(mine, theirs, lo):
     length = lo.shape[2]
     half = length // 2
+    own = half // 4
     part = lambda p: pl.BlockSpec((1, HD, half), unit_block(p))
-    unit = lambda rows, n: pl.BlockSpec((1, rows, n), lambda u, c: (u, 0, 0))
+    unit = lambda rows, n: pl.BlockSpec((1, rows, n), lambda u: (u, 0, 0))
+    heads = 4 * 3 * HD
+    dma = pltpu.SemaphoreType.DMA
     return pl.pallas_call(
         attend_kernel,
-        grid_spec=pltpu.PrefetchScalarGridSpec(
-            num_scalar_prefetch=1,
-            grid=(UNITS,),
-            in_specs=[part(0), part(1), part(2)] * 2
-            + [pl.BlockSpec((1, 1, length), lambda u, c: (u // 3, 0, 0))],
-            out_specs=[unit(HD, half), unit(HD, half), unit(1, length), unit(HD, length)],
-            scratch_shapes=[
-                pltpu.VMEM((HD, length), low),
-                pltpu.VMEM((length, HD), low),
-                pltpu.VMEM((HD, length), low),
-                pltpu.VMEM((WIN + QB, QB), full),
-            ],
-        ),
-        out_shape=[jax.ShapeDtypeStruct((UNITS, HD, half), low)] * 2
-        + [
+        grid=(UNITS,),
+        in_specs=[part(0), part(1), part(2)] * 2
+        + [pl.BlockSpec((1, 1, length), lambda u: (u // 3, 0, 0))],
+        out_specs=[pl.BlockSpec(memory_space=pl.ANY), unit(1, length), unit(HD, length)],
+        scratch_shapes=[
+            pltpu.VMEM((HD, length), low),
+            pltpu.VMEM((length, HD), low),
+            pltpu.VMEM((HD, length), low),
+            pltpu.VMEM((WIN + QB, QB), full),
+            pltpu.VMEM((UNITS, HD, length), low),
+            dma((7, UNITS)),
+            dma((7, UNITS)),
+            dma((UNITS,)),
+        ],
+        out_shape=[
+            jax.ShapeDtypeStruct((heads, 3 * own), low),
             jax.ShapeDtypeStruct((UNITS, 1, length), full),
             jax.ShapeDtypeStruct((UNITS, HD, length), full),
         ],
-        compiler_params=pltpu.CompilerParams(vmem_limit_bytes=40 << 20),
+        compiler_params=pltpu.CompilerParams(
+            vmem_limit_bytes=40 << 20, collective_id=1, has_side_effects=True
+        ),
         cost_estimate=pl.CostEstimate(
             flops=UNITS * 18 * 2 * 256 * 1024 * 128, bytes_accessed=20 << 20, transcendentals=0
         ),
         name="attend",
-    )(c, mine, mine, mine, theirs, theirs, theirs, lo)
+    )(mine, mine, mine, theirs, theirs, theirs, lo)
 
 
 def attend_back_kernel(
-    c_ref, qm, km, vm, gm, qt, kt, vt, gt, lo_ref, lse_ref, of_ref, dm, dt,
-    qs, ks, kts, vs, gs, grow, qrow, delta, dqs, dks, dvs,
+    qm, km, vm, qt, kt, vt, lo_ref, lse_ref, of_ref, norm_ref, gatt, dall, gw,
+    qs, ks, kts, vs, gs, grow, qrow, delta, dqs, dbuf, gsem, grsem, glsem, ssem, rsem, lsem,
 ):
-    c = c_ref[0]
+    u = pl.program_id(0)
+    c, t = place()
     length = lo_ref.shape[2]
     half = length // 2
-    for place, q, k, v, g in ((c, qm, km, vm, gm), (1 - c, qt, kt, vt, gt)):
-        off = pl.multiple_of(place * half, half)
+    own = half // 4
+    groups = ((0, 3), (3, 2))
+
+    def fetch(group, i, receiving):
+        dc, r = PEERS[i]
+        first, count = groups[group]
+        to_c, to_t = (c ^ dc, t ^ r)
+        seq = 2 * to_c if group == 0 else 1
+        head = to_t * 3 + (0 if group == 0 else to_c)
+        src = gatt.at[pl.ds(head, count), :, pl.ds(pl.multiple_of(seq * own, own), own)]
+        dst = gs.at[pl.ds(first, count), :, pl.ds(pl.multiple_of((c * 4 + t) * own, own), own)]
+        if i == 0:
+            return pltpu.make_async_copy(src, dst, glsem.at[group])
+        return pltpu.make_async_remote_copy(
+            src, dst, gsem.at[i - 1, group], grsem.at[i - 1, group], device_id=at_peer(c, t, dc, r)
+        )
+
+    @pl.when(u == 0)
+    def _():
+        greet(c, t)
+        gw[...] = jnp.zeros_like(gw)
+        greeted()
+        for group in range(2):
+            for i in range(1, len(PEERS)):
+                fetch(group, i, False).start()
+            fetch(group, 0, False).start()
+
+    for group in range(2):
+
+        @pl.when(u == groups[group][0])
+        def _():
+            fetch(group, 0, True).wait()
+            for i in range(1, len(PEERS)):
+                fetch(group, i, True).wait_recv()
+
+    for core, q, k, v in ((c, qm, km, vm), (1 - c, qt, kt, vt)):
+        off = pl.multiple_of(core * half, half)
         scaled = q[0] * low(0.125)
+        g = gs[u, :, pl.ds(off, half)]
         qs[:, pl.ds(off, half)] = scaled
         kts[:, pl.ds(off, half)] = k[0]
-        gs[:, pl.ds(off, half)] = g[0]
         ks[pl.ds(off, half), :] = k[0].T
         vs[pl.ds(off, half), :] = v[0].T
-        grow[pl.ds(off, half), :] = g[0].T
+        grow[pl.ds(off, half), :] = g.T
         qrow[pl.ds(off, half), :] = scaled.T
         delta[:, pl.ds(off, half)] = jnp.sum(
-            g[0].astype(full) * of_ref[0, :, pl.ds(off, half)], axis=0, keepdims=True
+            g.astype(full) * of_ref[0, :, pl.ds(off, half)], axis=0, keepdims=True
         )
     dqs[...] = jnp.zeros_like(dqs)
     for key_start in range(0, length, QB):
@@ -186,50 +306,99 @@
             if start == key_start:
                 allowed &= key_pos <= start + lax.broadcasted_iota(jnp.int32, (QB, QB), 1)
             p = jnp.exp(jnp.where(allowed, s, NEG))
-            dp = nn(v, gs[:, cols])
+            dp = nn(v, gs[u, :, cols])
             ds = (p * (dp - delta[:, cols])).astype(low)
             dv += nn(p.astype(low), grow[cols, :])
             dk += nn(ds, qrow[cols, :])
             dqs[:, cols] += nn(key_t, ds)
-        dks[:, rows] = dk.T.astype(low)
-        dvs[:, rows] = dv.T.astype(low)
-    for ref, place in ((dm, c), (dt, 1 - c)):
-        off = pl.ds(pl.multiple_of(place * half, half), half)
-        ref[0, 0] = (dqs[:, off] * 0.125).astype(low)
-        ref[0, 1] = dks[:, off]
-        ref[0, 2] = dvs[:, off]
-
-
-def attend_back(c, mine, theirs, grad_mine, grad_theirs, lo, lse, attended):
+        dbuf[u, 1, :, rows] = dk.T.astype(low)
+        dbuf[u, 2, :, rows] = dv.T.astype(low)
+    dbuf[u, 0] = (dqs[...] * 0.125).astype(low)
+
+    def move(unit, i, source_core):
+        dc, r = PEERS[i]
+        h, seq = unit_place(unit, source_core)
+        dest = pl.multiple_of(((c ^ dc) * 4 + (t ^ r)) * own, own)
+        src = dbuf.at[unit, :, :, pl.ds(dest, own)]
+        dst = dall.at[:, t * 3 + h, :, pl.ds(pl.multiple_of(seq * own, own), own)]
+        if i == 0:
+            return pltpu.make_async_copy(src, dst, lsem.at[unit])
+        return pltpu.make_async_remote_copy(
+            src, dst, ssem.at[i - 1, unit], rsem.at[i - 1, unit], device_id=at_peer(c, t, dc, r)
+        )
+
+    @pl.when(sends(u, c))
+    def _():
+        for i in range(1, len(PEERS)):
+            move(u, i, c).start()
+        move(u, 0, c).start()
+        h, _ = unit_place(u, c)
+        gw[h] += nn(dbuf[u].reshape(3 * HD, length), norm_ref[0])
+
+    @pl.when(u == pl.num_programs(0) - 1)
+    def _():
+        for group in range(2):
+            for i in range(1, len(PEERS)):
+                fetch(group, i, False).wait_send()
+        for unit in range(UNITS):
+            for i, (dc, r) in enumerate(PEERS):
+
+                @pl.when(sends(unit, c))
+                def _():
+                    if i:
+                        move(unit, i, c).wait_send()
+                    else:
+                        move(unit, i, c).wait()
+
+                if i:
+
+                    @pl.when(sends(unit, c ^ dc))
+                    def _():
+                        move(unit, i, c ^ dc).wait_recv()
+
+
+def attend_back(mine, theirs, grad_attended, lo, lse, attended, normed):
     length = lo.shape[2]
     half = length // 2
+    own = half // 4
+    width = normed.shape[2]
     part = lambda p: pl.BlockSpec((1, HD, half), unit_block(p))
-    unit = lambda rows, n: pl.BlockSpec((1, rows, n), lambda u, c: (u, 0, 0))
+    unit = lambda rows, n: pl.BlockSpec((1, rows, n), lambda u: (u, 0, 0))
     wide, tall = pltpu.VMEM((HD, length), low), pltpu.VMEM((length, HD), low)
+    dma = pltpu.SemaphoreType.DMA
     return pl.pallas_call(
         attend_back_kernel,
-        grid_spec=pltpu.PrefetchScalarGridSpec(
-            num_scalar_prefetch=1,
-            grid=(UNITS,),
-            in_specs=[part(0), part(1), part(2), unit(HD, half)] * 2
-            + [
-                pl.BlockSpec((1, 1, length), lambda u, c: (u // 3, 0, 0)),
-                unit(1, length),
-                unit(HD, length),
-            ],
-            out_specs=[pl.BlockSpec((1, 3, HD, half), lambda u, c: (u, 0, 0, 0))] * 2,
-            scratch_shapes=[
-                wide, tall, wide, tall, wide, tall, tall,
-                pltpu.VMEM((1, length), full), pltpu.VMEM((HD, length), full), wide, wide,
-            ],
+        grid=(UNITS,),
+        in_specs=[part(0), part(1), part(2)] * 2
+        + [
+            pl.BlockSpec((1, 1, length), lambda u: (u // 3, 0, 0)),
+            unit(1, length),
+            unit(HD, length),
+            pl.BlockSpec((1, length, width), lambda u: (u // 3, 0, 0)),
+            pl.BlockSpec(memory_space=pl.ANY),
+        ],
+        out_specs=[
+            pl.BlockSpec(memory_space=pl.ANY),
+            pl.BlockSpec((3, 3 * HD, width), lambda u: (0, 0, 0)),
+        ],
+        scratch_shapes=[
+            wide, tall, wide, tall, pltpu.VMEM((UNITS, HD, length), low), tall, tall,
+            pltpu.VMEM((1, length), full), pltpu.VMEM((HD, length), full),
+            pltpu.VMEM((UNITS, 3, HD, length), low),
+            dma((7, 2)), dma((7, 2)), dma((2,)), dma((7, UNITS)), dma((7, UNITS)), dma((UNITS,)),
+        ],
+        out_shape=[
+            jax.ShapeDtypeStruct((3, 12, HD, 3 * own), low),
+            jax.ShapeDtypeStruct((3, 3 * HD, width), full),
+        ],
+        compiler_params=pltpu.CompilerParams(
+            vmem_limit_bytes=50 << 20, collective_id=2, has_side_effects=True
         ),
-        out_shape=[jax.ShapeDtypeStruct((UNITS, 3, HD, half), low)] * 2,
-        compiler_params=pltpu.CompilerParams(vmem_limit_bytes=40 << 20),
         cost_estimate=pl.CostEstimate(
             flops=UNITS * 18 * 5 * 256 * 1024 * 128, bytes_accessed=30 << 20, transcendentals=0
         ),
         name="attend_back",
-    )(c, mine, mine, mine, grad_mine, theirs, theirs, theirs, grad_theirs, lo, lse, attended)
+    )(mine, mine, mine, theirs, theirs, theirs, lo, lse, attended, normed, grad_attended)
 
 
 def gelu_and_slope(v):
@@ -356,6 +525,10 @@
     w_proj = jnp.stack(gather_tensor(w_out.T, 0), axis=0)
     w_proj = gather_dp(w_proj, 1)
 
+    w_attn_all = jnp.stack(gather_tensor(w_attn.T, 0)).reshape(4, 3, local, width)
+    w_attn_all = [lax.dynamic_index_in_dim(w_attn_all, t ^ p, 0, False) for p in range(4)]
+    w_attn_all = jnp.stack(w_attn_all, axis=1).reshape(12 * local, width)
+
     lo = jnp.zeros((sequences, length), jnp.int32)
     for value in range(8):
         before = jnp.sum((segments < value).astype(jnp.int32), axis=1, keepdims=True)
@@ -381,31 +554,23 @@
         whole, shared = (a.reshape(-1, HD, span) for a in (whole, shared))
         return jnp.concatenate([whole, shared], axis=0)
 
-    def rejoin(mine, theirs):
-        first = jnp.where(c == 0, mine[:3], theirs[:3])
-        last = jnp.where(c == 0, theirs[:3], mine[:3])
-        shared = jnp.where(
-            c == 0,
-            jnp.concatenate([mine[3:5], theirs[4:5]]),
-            jnp.concatenate([theirs[3:4], mine[3:5]]),
-        )
-        return jnp.stack([first, shared, last])
-
-    core = c.reshape(1).astype(jnp.int32)
     qkv_mine = units(projected, 3, c)
     qkv_theirs = across(units(projected, 3, 1 - c), "context", 1)
-    out_mine, out_sent, log_totals, out_full = attend(core, qkv_mine, qkv_theirs, lo)
-    heads_out = rejoin(out_mine, across(out_sent, "context", 1))
-    heads_out = heads_out.reshape(sequences, local, span)
-
-    def to_owner(array, by):
-        piece = lax.dynamic_slice_in_dim(array, (t ^ by) * own, own, 2)
-        return across(piece, "tensor", by) if by else piece
-
-    attended = jnp.stack([to_owner(heads_out, r) for r in range(4)])
-    attended = attended.transpose(0, 2, 1, 3).reshape(4 * local, rows)
-
-    proj_rows = w_proj.transpose(0, 2, 1).reshape(4 * local, width)
+    attended, log_totals, out_full = attend(qkv_mine, qkv_theirs, lo)
+
+    def two_sequences(core):
+        whole = lax.dynamic_slice_in_dim(normed_one, 2 * core * span, span, 0)
+        return jnp.stack([whole, normed_one[span : 2 * span]])
+
+    normed_theirs = across(two_sequences(1 - c), "context", 1)
+    normed_mine = two_sequences(c)
+    normed_units = jnp.where(
+        c == 0,
+        jnp.concatenate([normed_mine, normed_theirs], axis=1),
+        jnp.concatenate([normed_theirs, normed_mine], axis=1),
+    )
+
+    proj_rows = jnp.stack(in_order(w_proj.transpose(0, 2, 1))).reshape(4 * local, width)
     inputs = tokens.astype(full).reshape(rows, width)
     middle = inputs + tn(attended, proj_rows)
     inv_two = inverse(middle)
@@ -425,18 +590,12 @@
     grad_middle = cot.astype(full) + norm_back(grad_norm_two, gain_second, middle, inv_two)
     grad_low = grad_middle.astype(low)
     grad_proj = nn(attended, grad_low)
-    grad_att = nt(proj_rows, grad_low).astype(low).reshape(4, local, sequences, own)
-    grad_heads = jnp.stack([across(grad_att[r], "tensor", r) if r else grad_att[0] for r in range(4)])
-    grad_heads = jnp.stack(in_order(grad_heads), axis=2).reshape(local, sequences * span)
-    g_mine = units(grad_heads, 1, c)
-    g_theirs = across(units(grad_heads, 1, 1 - c), "context", 1)
-    d_mine, d_sent = attend_back(core, qkv_mine, qkv_theirs, g_mine, g_theirs, lo, log_totals, out_full)
-    grad_projected = rejoin(d_mine, across(d_sent, "context", 1))
-    grad_projected = grad_projected.transpose(2, 1, 3, 0, 4).reshape(3 * local, sequences * span)
-    grad_attn = nn(grad_projected, normed_one)
-    spread = dot(grad_projected, w_attn, ((0,), (1,))).reshape(sequences, 4, own, width)
-    spread = [lax.dynamic_index_in_dim(spread, t ^ r, 1, False) for r in range(4)]
-    grad_norm_one = scatter_tensor(spread, 1).reshape(rows, width)
+    grad_att = nt(proj_rows, grad_low).astype(low).reshape(4 * heads, HD, rows)
+    grad_projected, grad_attn = attend_back(
+        qkv_mine, qkv_theirs, grad_att, lo, log_totals, out_full, normed_units
+    )
+    grad_attn = grad_attn.reshape(heads, 3, HD, width).transpose(1, 0, 2, 3).reshape(3 * local, width)
+    grad_norm_one = tn(grad_projected.reshape(12 * local, rows), w_attn_all)
     inv_one = inverse(inputs)
     grad_input = grad_middle + norm_back(grad_norm_one, gain_first, inputs, inv_one)
 
@@ -463,7 +622,8 @@
     own_up = swap_halves(up_down[0], 1).astype(full)
     own_down = swap_halves(up_down[1].T, 0).astype(full)
     proj = half_sum(grad_proj.reshape(4, local, width), 1)
-    proj = scatter_dp(scatter_tensor([proj[r] for r in range(4)], 0), 1)
+    proj = [lax.dynamic_index_in_dim(proj, t ^ r, 0, False) for r in range(4)]
+    proj = scatter_dp(scatter_tensor(proj, 0), 1)
     own_proj = swap_halves(proj, 0).astype(full)
     attn = scatter_dp(half_sum(grad_attn, 0), 1).T
     own_attn = swap_halves(attn, 1).astype(full)

time: 579 us -> 531 us (0.917)
  waiting for transfers between devices: 217 us -> 140 us
  Pallas kernels: 100 us -> 147 us
  local copies, waits for them, and re-layouts: 63.3 us -> 31.9 us
  starting transfers between devices: 80.4 us -> 109 us
  other arithmetic: 69.8 us -> 59.4 us
  matrix products: 20.7 us -> 11.2 us
    ppermute x62 -> x56, waiting for transfers between devices: 180 us -> 97.7 us  [across(): lax.ppermute(array, axis, [(i, i ^ by) for i in range(lax.axis_size(axis))])]
    pallas_call x2, Pallas kernels: 67.1 us -> 114 us  [the longest x1 85.4 us: attend_back(): pl.pallas_call(attend_back_kernel, grid=(UNITS,), in_specs=[part(0), part...]
    ppermute x62 -> x56, starting transfers between devices: 80.3 us -> 109 us  [across(): lax.ppermute(array, axis, [(i, i ^ by) for i in range(lax.axis_size(axis))])]
    reduce_scatter x1, waiting for transfers between devices: 0.02 us -> 28.1 us  [scatter_dp(): lax.psum_scatter(array.astype(low), 'dp', scatter_dimension=axis, tiled=T...]
    unnamed x5, waiting for transfers between devices: 37.1 us -> 14.6 us
    dot_general x2 -> x0, local copies, waits for them, and re-layouts: 10.3 us -> none  [dot(): lax.dot_general(left, right, (dims, ((), ())), preferred_element_type=full)]
    dot_general x6 -> x5, matrix products: 20.7 us -> 11.2 us  [dot(): lax.dot_general(left, right, (dims, ((), ())), preferred_element_type=full)]
    squeeze x4 -> x0, local copies, waits for them, and re-layouts: 7.37 us -> none  [the longest x3 5.51 us: per_device(): grad_att[r]]
  transfers between devices with their start and end apart: 65 -> 59, of which waited for: 23 -> 20; matrix products, arithmetic and copies ran while one was open for 24% -> 17% of each run, Pallas kernels for 12% -> 28%
where the time goes in v3:
time: 531 us; the launch traced here: 521 us
  Pallas kernels  147 us (28%)
  waiting for transfers between devices  140 us (26%)
  starting transfers between devices  109 us (21%)
  other arithmetic  59.4 us (11%)
  local copies, waits for them, and re-layouts  31.9 us (6%)
  between operations  15.1 us (3%)
  matrix products  11.2 us (2%)
  blocking collectives  7.77 us (1%)
    ppermute x56, starting transfers between devices, across(): lax.ppermute(array, axis, [(i, i ^ by) for i in range(lax.axis_size(axis))])  109 us
    ppermute x56, waiting for transfers between devices, across(): lax.ppermute(array, axis, [(i, i ^ by) for i in range(lax.axis_size(axis))])  97.7 us
    pallas_call x1, Pallas kernels, attend_back(): pl.pallas_call(attend_back_kernel, grid=(UNITS,), in_specs=[part(0), part...  85.4 us
    pallas_call x1, Pallas kernels, feed(): pl.pallas_call(feed_kernel, grid=(pieces // 2,), in_specs=[whole] * 4 + [...  33.1 us
    pallas_call x1, Pallas kernels, attend(): pl.pallas_call(attend_kernel, grid=(UNITS,), in_specs=[part(0), part(1),...  28.2 us
    reduce_scatter x1, waiting for transfers between devices, scatter_dp(): lax.psum_scatter(array.astype(low), 'dp', scatter_dimension=axis, tiled=T...  28.1 us
    unnamed x93, local copies, waits for them, and re-layouts  16.3 us
    unnamed x5, waiting for transfers between devices  14.6 us
  transfers between devices with their start and end apart: 59, of which 20 were waited for; matrix products, arithmetic and copies ran while one was open for 17% of the time, Pallas kernels for 28%

profile of v3, /device:TPU:1, one launch (start us, length us, event | category | flops | bytes accessed | tf_op | source)
XLA Modules:
  0.0 521.5 jit_solution(13871652383320186098)
XLA Ops:
  22.7 2.8 collective-permute-done.13
  43.3 4.2 collective-permute-done.2
  57.2 25.9 %collective-permute-done.20 = bf16[4,192,192]{1,2,0:T(8,128)(2,1)S(1)} collective-permute-done((bf16[4,192,192]{1,2,0:T(8,128)(2,1)S(1)}, bf16[4,192,192]{1,2,0:T(8,128)(2,1)S(1)}, u32[]{:S(2)}, u32[]{:S(2)}) %collective-permute-start.20) | collective-permute-done | bytes 294944 | tf_op jit(solution)/shard_map/ppermute | solution.py:38
  91.8 13.3 %collective-permute-start.23 = (bf16[3,256,768]{2,1,0:T(8,128)(2,1)}, bf16[3,256,768]{2,1,0:T(8,128)(2,1)}, u32[]{:S(2)}, u32[]{:S(2)}) collective-permute-start(bf16[3,256,768]{2,1,0:T(8,128)(2,1)} %param.17), channel_id=1, source_target_pairs={{0,4},{4,0},{1,5},{5,1},{2,6},{6,2},{3,7},{7,3},{8,12},{12,8},{9,1... | collective-permute-start | bytes 3538952 | tf_op jit(solution)/shard_map/ppermute | solution.py:38
  105.2 10.4 %collective-permute-start.30 = (bf16[2,4,192,384]{3,2,0,1:T(8,128)(2,1)}, bf16[2,4,192,384]{3,2,0,1:T(8,128)(2,1)}, u32[]{:S(2)}, u32[]{:S(2)}) collective-permute-start(bf16[2,4,192,384]{3,2,0,1:T(8,128)(2,1)} %get-tuple-element.105), channel_id=1, source_target_pairs={{0,8},{8,0},{16,24},{24,16},{1,9},{9,1},{17,25},{25,17},{2,10},{10... | collective-permute-start | bytes 3538952 | tf_op jit(solution)/shard_map/ppermute | solution.py:38
  124.5 3.2 convolution_convert_fusion
  128.4 13.5 %collective-permute-start.12 = (bf16[15,64,1024]{2,1,0:T(8,128)(2,1)S(1)}, bf16[15,64,1024]{2,1,0:T(8,128)(2,1)S(1)}, u32[]{:S(2)}, u32[]{:S(2)}) collective-permute-start(bf16[15,64,1024]{2,1,0:T(8,128)(2,1)S(1)} %pad_maximum_fusion.7), channel_id=1, source_target_pairs={{0,4},{4,0},{1,5},{5,1},{2,6},{6,2},{3,7},{7,3},{8,12},{12,8},{9,1... | collective-permute-start | bytes 5898248 | tf_op jit(solution)/shard_map/ppermute | solution.py:38
  144.3 14.4 %collective-permute-done.30 = bf16[2,4,192,384]{3,2,0,1:T(8,128)(2,1)} collective-permute-done((bf16[2,4,192,384]{3,2,0,1:T(8,128)(2,1)}, bf16[2,4,192,384]{3,2,0,1:T(8,128)(2,1)}, u32[]{:S(2)}, u32[]{:S(2)}) %collective-permute-start.30) | collective-permute-done | bytes 1179680 | tf_op jit(solution)/shard_map/ppermute | solution.py:38
  163.2 24.1 %collective-permute-done.32 = bf16[2,4,192,384]{3,2,0,1:T(8,128)(2,1)} collective-permute-done((bf16[2,4,192,384]{3,2,0,1:T(8,128)(2,1)}, bf16[2,4,192,384]{3,2,0,1:T(8,128)(2,1)}, u32[]{:S(2)}, u32[]{:S(2)}) %collective-permute-start.32) | collective-permute-done | bytes 1179680 | tf_op jit(solution)/shard_map/ppermute | solution.py:38
  187.3 20.4 %collective-permute-start.35 = (bf16[2,1024,768]{2,1,0:T(8,128)(2,1)}, bf16[2,1024,768]{2,1,0:T(8,128)(2,1)}, u32[]{:S(2)}, u32[]{:S(2)}) collective-permute-start(bf16[2,1024,768]{2,1,0:T(8,128)(2,1)} %pad_maximum_fusion.5), channel_id=1, source_target_pairs={{0,4},{4,0},{1,5},{5,1},{2,6},{6,2},{3,7},{7,3},{8,12},{12,8},{9,1... | collective-permute-start | bytes 9437192 | tf_op jit(solution)/shard_map/ppermute | solution.py:38
  211.7 28.2 %attend.1 = (bf16[768,768]{1,0:T(8,128)(2,1)S(1)}, f32[5,1,2048]{2,1,0:T(1,128)S(1)}, f32[5,64,2048]{2,1,0:T(8,128)S(1)}) custom-call(bf16[15,64,1024]{2,1,0:T(8,128)(2,1)S(1)} %pad_maximum_fusion.6.qm.km.vm, bf16[15,64,1024]{2,1,0:T(8,128)(2,1)S(1)} %pad_maximum_fusion.6.qm.km.vm, bf16[15,64,1024]{2,1,0:T(8,128)(2,1)S(1)} %pad_maximum_fusion.6.qm.km.vm, ...), custom_call_target="tpu_custom_call" | custom-call | flops 6039797760 | bytes 20971520 | tf_op jit(solution)/shard_map/attend/pallas_call | solution.py:208
  246.3 7.5 %maximum_select_fusion.norm_ref = bf16[2,2048,768]{2,1,0:T(8,128)(2,1)} fusion(bf16[2,1024,768]{2,1,0:T(8,128)(2,1)} %collective-permute-done.35, bf16[1,1024,768]{2,1,0:T(8,128)(2,1)S(1)} %get-tuple-element.62, bf16[1,1024,768]{2,1,0:T(8,128)(2,1)S(1)} %get-tuple-element.60, pred[]{:T(512)S(6)} %eq.32), kind=kLoop, calls=%fused_computation.4 | loop fusion | flops 40894464 | bytes 12582913 | tf_op jit(solution)/shard_map/jit(_where)/select_n | solution.py:567
  254.8 33.1 %feed.1 = (f32[768,768]{1,0:T(8,128)}, bf16[768,768]{1,0:T(8,128)(2,1)}, f32[768,768]{1,0:T(8,128)}, bf16[768,768]{1,0:T(8,128)(2,1)}, bf16[4,768,384]{2,1,0:T(8,128)(2,1)}, /*index=5*/bf16[4,768,384]{2,1,0:T(8,128)(2,1)}) custom-call(bf16[768,768]{1,0:T(8,128)(2,1)} %copy-done.30, bf16[768,768]{1,0:T(8,128)(2,1)} %copy-done.41, ...), custom_call_target="tpu_custom_call" | custom-call | flops 21743271936 | bytes 20971520 | tf_op jit(solution)/shard_map/feed/pallas_call | solution.py:482
  299.9 3.3 multiply_add_fusion
  307.0 85.4 %attend_back.1 = (bf16[3,12,64,768]{3,2,1,0:T(8,128)(2,1)}, f32[3,192,768]{2,1,0:T(8,128)S(1)}) custom-call(bf16[15,64,1024]{2,1,0:T(8,128)(2,1)} %copy-done.2, bf16[15,64,1024]{2,1,0:T(8,128)(2,1)} %copy-done.2, bf16[15,64,1024]{2,1,0:T(8,128)(2,1)} %copy-done.2, bf16[15,64,1024]{2,1,0:T(8,128)(2,1)} %copy-done.3, bf16[15,64,1024]{2,1,0:T(8,128)(2,1)} %copy-done.3, ...), custom_call_target="tpu_custom_call" | custom-call | flops 15099494400 | bytes 31457280 | tf_op jit(solution)/shard_map/attend_back/pallas_call | solution.py:369
  394.1 2.9 convert_element_type.228
  401.1 6.2 %collective-permute-done.47 = bf16[2,48,768]{2,1,0:T(8,128)(2,1)S(1)} collective-permute-done((bf16[2,48,768]{2,1,0:T(8,128)(2,1)S(1)}, bf16[2,48,768]{2,1,0:T(8,128)(2,1)S(1)}, u32[]{:S(2)}, u32[]{:S(2)}) %collective-permute-start.47) | collective-permute-done | bytes 147488 | tf_op jit(solution)/shard_map/ppermute | solution.py:38
  411.9 3.7 collective-permute-start.42
  427.0 8.7 %collective-permute-done.51 = bf16[2,384,384]{2,1,0:T(8,128)(2,1)} collective-permute-done((bf16[2,384,384]{2,1,0:T(8,128)(2,1)}, bf16[2,384,384]{2,1,0:T(8,128)(2,1)}, u32[]{:S(2)}, u32[]{:S(2)}) %collective-permute-start.51) | collective-permute-done | bytes 589856 | tf_op jit(solution)/shard_map/ppermute | solution.py:38
  443.5 4.5 fusion.3
  450.3 3.2 fusion.7
  454.3 14.6 %reduce-scatter.10.cloned.1.call-done = bf16[192,288]{1,0:T(8,128)(2,1)} async-done(((bf16[768,288]{1,0:T(8,128)(2,1)}), bf16[192,288]{1,0:T(8,128)(2,1)}) %reduce-scatter.10.cloned.1.call-update) | async-done | bytes 110608
  472.6 28.1 %reduce-scatter.8.cloned.1.call-done = bf16[2,192,384]{2,1,0:T(8,128)(2,1)} async-done(((bf16[2,768,384]{2,1,0:T(8,128)(2,1)}), bf16[2,192,384]{2,1,0:T(8,128)(2,1)}) %reduce-scatter.8.cloned.1.call-update) | async-done | bytes 294928 | tf_op jit(solution)/shard_map/reduce_scatter | solution.py:603
  504.9 7.8 %all-reduce = (f32[192]{0:T(256)S(1)}, f32[192]{0:T(256)S(1)}) all-reduce(f32[192]{0:T(256)S(1)} %multiply_reduce_fusion.4, f32[192]{0:T(256)S(1)} %get-tuple-element.58), channel_id=1, replica_groups=mesh['dp'=4,'context'=2,'tensor'=4] {'tensor'}, use_global_device_ids=true, to_apply=%region_17.18 | all-reduce | flops 384 | bytes 3072 | tf_op jit(solution)/shard_map/psum | solution.py:633
  (312 shorter events, 136.9 us)
Async XLA Ops:
  7.2 440.8 %reduce-scatter.12.cloned.1.call-start = ((), (), s32[]{:S(2)}) async-start(), calls=%async_computation.5 | async-start | bytes 245760
  36.6 46.4 %collective-permute-start.20 = (bf16[4,192,192]{1,2,0:T(8,128)(2,1)S(1)}, bf16[4,192,192]{1,2,0:T(8,128)(2,1)S(1)}, u32[]{:S(2)}, u32[]{:S(2)}) collective-permute-start(bf16[4,192,192]{1,2,0:T(8,128)(2,1)S(1)} %get-tuple-element.121), channel_id=1, source_target_pairs={{0,16},{8,24},{16,0},{24,8},{1,17},{9,25},{17,1},{25,9},{2,18},{10... | collective-permute-start | bytes 884744 | tf_op jit(solution)/shard_map/ppermute | solution.py:38
  39.8 44.2 %collective-permute-start.21 = (bf16[4,192,192]{1,2,0:T(8,128)(2,1)S(1)}, bf16[4,192,192]{1,2,0:T(8,128)(2,1)S(1)}, u32[]{:S(2)}, u32[]{:S(2)}) collective-permute-start(bf16[4,192,192]{1,2,0:T(8,128)(2,1)S(1)} %get-tuple-element.121), channel_id=1, source_target_pairs={{0,24},{8,16},{16,8},{24,0},{1,25},{9,17},{17,9},{25,1},{2,26},{10... | collective-permute-start | bytes 884744 | tf_op jit(solution)/shard_map/ppermute | solution.py:38
  50.8 35.8 %collective-permute-start.6 = (bf16[3,128,768]{2,1,0:T(8,128)(2,1)S(1)}, bf16[3,128,768]{2,1,0:T(8,128)(2,1)S(1)}, u32[]{:S(2)}, u32[]{:S(2)}) collective-permute-start(bf16[3,128,768]{2,1,0:T(8,128)(2,1)S(1)} %copy-done.34), channel_id=1, source_target_pairs={{0,2},{1,3},{2,0},{3,1},{4,6},{5,7},{6,4},{7,5},{8,10},{9,11},{10,... | collective-permute-start | bytes 1769480 | tf_op jit(solution)/shard_map/ppermute | solution.py:38
  52.0 35.1 %collective-permute-start.4 = (bf16[3,128,768]{2,1,0:T(8,128)(2,1)S(1)}, bf16[3,128,768]{2,1,0:T(8,128)(2,1)S(1)}, u32[]{:S(2)}, u32[]{:S(2)}) collective-permute-start(bf16[3,128,768]{2,1,0:T(8,128)(2,1)S(1)} %copy-done.34), channel_id=1, source_target_pairs={{0,1},{1,0},{2,3},{3,2},{4,5},{5,4},{6,7},{7,6},{8,9},{9,8},{10,11... | collective-permute-start | bytes 1769480 | tf_op jit(solution)/shard_map/ppermute | solution.py:38
  54.4 32.1 %collective-permute-start.3 = (bf16[3,128,768]{2,1,0:T(8,128)(2,1)S(1)}, bf16[3,128,768]{2,1,0:T(8,128)(2,1)S(1)}, u32[]{:S(2)}, u32[]{:S(2)}) collective-permute-start(bf16[3,128,768]{2,1,0:T(8,128)(2,1)S(1)} %get-tuple-element.112), channel_id=1, source_target_pairs={{0,1},{1,0},{2,3},{3,2},{4,5},{5,4},{6,7},{7,6},{8,9},{9,8},{10,11... | collective-permute-start | bytes 1769480 | tf_op jit(solution)/shard_map/ppermute | solution.py:38
  86.6 31.0 %collective-permute-start.7 = (bf16[3,128,768]{2,1,0:T(8,128)(2,1)S(1)}, bf16[3,128,768]{2,1,0:T(8,128)(2,1)S(1)}, u32[]{:S(2)}, u32[]{:S(2)}) collective-permute-start(bf16[3,128,768]{2,1,0:T(8,128)(2,1)S(1)} %collective-permute-done.3), channel_id=1, source_target_pairs={{0,2},{1,3},{2,0},{3,1},{4,6},{5,7},{6,4},{7,5},{8,10},{9,11},{10,... | collective-permute-start | bytes 1769480 | tf_op jit(solution)/shard_map/ppermute | solution.py:38
  87.1 32.6 %collective-permute-start.8 = (bf16[3,128,768]{2,1,0:T(8,128)(2,1)S(1)}, bf16[3,128,768]{2,1,0:T(8,128)(2,1)S(1)}, u32[]{:S(2)}, u32[]{:S(2)}) collective-permute-start(bf16[3,128,768]{2,1,0:T(8,128)(2,1)S(1)} %collective-permute-done.6), channel_id=1, source_target_pairs={{0,1},{1,0},{2,3},{3,2},{4,5},{5,4},{6,7},{7,6},{8,9},{9,8},{10,11... | collective-permute-start | bytes 1769480 | tf_op jit(solution)/shard_map/ppermute | solution.py:38
  91.8 162.0 %collective-permute-start.23 = (bf16[3,256,768]{2,1,0:T(8,128)(2,1)}, bf16[3,256,768]{2,1,0:T(8,128)(2,1)}, u32[]{:S(2)}, u32[]{:S(2)}) collective-permute-start(bf16[3,256,768]{2,1,0:T(8,128)(2,1)} %param.17), channel_id=1, source_target_pairs={{0,4},{4,0},{1,5},{5,1},{2,6},{6,2},{3,7},{7,3},{8,12},{12,8},{9,1... | collective-permute-start | bytes 3538952 | tf_op jit(solution)/shard_map/ppermute | solution.py:38
  105.2 53.5 %collective-permute-start.30 = (bf16[2,4,192,384]{3,2,0,1:T(8,128)(2,1)}, bf16[2,4,192,384]{3,2,0,1:T(8,128)(2,1)}, u32[]{:S(2)}, u32[]{:S(2)}) collective-permute-start(bf16[2,4,192,384]{3,2,0,1:T(8,128)(2,1)} %get-tuple-element.105), channel_id=1, source_target_pairs={{0,8},{8,0},{16,24},{24,16},{1,9},{9,1},{17,25},{25,17},{2,10},{10... | collective-permute-start | bytes 3538952 | tf_op jit(solution)/shard_map/ppermute | solution.py:38
  115.6 45.4 %collective-permute-start.31 = (bf16[2,4,192,384]{3,2,0,1:T(8,128)(2,1)}, bf16[2,4,192,384]{3,2,0,1:T(8,128)(2,1)}, u32[]{:S(2)}, u32[]{:S(2)}) collective-permute-start(bf16[2,4,192,384]{3,2,0,1:T(8,128)(2,1)} %get-tuple-element.105), channel_id=1, source_target_pairs={{0,16},{8,24},{16,0},{24,8},{1,17},{9,25},{17,1},{25,9},{2,18},{10... | collective-permute-start | bytes 3538952 | tf_op jit(solution)/shard_map/ppermute | solution.py:38
  117.6 69.7 %collective-permute-start.32 = (bf16[2,4,192,384]{3,2,0,1:T(8,128)(2,1)}, bf16[2,4,192,384]{3,2,0,1:T(8,128)(2,1)}, u32[]{:S(2)}, u32[]{:S(2)}) collective-permute-start(bf16[2,4,192,384]{3,2,0,1:T(8,128)(2,1)} %get-tuple-element.105), channel_id=1, source_target_pairs={{0,24},{8,16},{16,8},{24,0},{1,25},{9,17},{17,9},{25,1},{2,26},{10... | collective-permute-start | bytes 3538952 | tf_op jit(solution)/shard_map/ppermute | solution.py:38
  128.4 83.3 %collective-permute-start.12 = (bf16[15,64,1024]{2,1,0:T(8,128)(2,1)S(1)}, bf16[15,64,1024]{2,1,0:T(8,128)(2,1)S(1)}, u32[]{:S(2)}, u32[]{:S(2)}) collective-permute-start(bf16[15,64,1024]{2,1,0:T(8,128)(2,1)S(1)} %pad_maximum_fusion.7), channel_id=1, source_target_pairs={{0,4},{4,0},{1,5},{5,1},{2,6},{6,2},{3,7},{7,3},{8,12},{12,8},{9,1... | collective-permute-start | bytes 5898248 | tf_op jit(solution)/shard_map/ppermute | solution.py:38
  158.7 233.8 %collective-permute-start.39 = (bf16[288,768]{1,0:T(8,128)(2,1)}, bf16[288,768]{1,0:T(8,128)(2,1)}, u32[]{:S(2)}, u32[]{:S(2)}) collective-permute-start(bf16[288,768]{1,0:T(8,128)(2,1)} %get-tuple-element.119), channel_id=1, source_target_pairs={{0,2},{1,3},{2,0},{3,1},{4,6},{5,7},{6,4},{7,5},{8,10},{9,11},{10,... | collective-permute-start | bytes 1327112 | tf_op jit(solution)/shard_map/ppermute | solution.py:38
  161.0 262.3 %collective-permute-start.38 = (bf16[288,768]{1,0:T(8,128)(2,1)}, bf16[288,768]{1,0:T(8,128)(2,1)}, u32[]{:S(2)}, u32[]{:S(2)}) collective-permute-start(bf16[288,768]{1,0:T(8,128)(2,1)} %get-tuple-element.118), channel_id=1, source_target_pairs={{0,2},{1,3},{2,0},{3,1},{4,6},{5,7},{6,4},{7,5},{8,10},{9,11},{10,... | collective-permute-start | bytes 1327112 | tf_op jit(solution)/shard_map/ppermute | solution.py:38
  187.3 59.0 %collective-permute-start.35 = (bf16[2,1024,768]{2,1,0:T(8,128)(2,1)}, bf16[2,1024,768]{2,1,0:T(8,128)(2,1)}, u32[]{:S(2)}, u32[]{:S(2)}) collective-permute-start(bf16[2,1024,768]{2,1,0:T(8,128)(2,1)} %pad_maximum_fusion.5), channel_id=1, source_target_pairs={{0,4},{4,0},{1,5},{5,1},{2,6},{6,2},{3,7},{7,3},{8,12},{12,8},{9,1... | collective-permute-start | bytes 9437192 | tf_op jit(solution)/shard_map/ppermute | solution.py:38
  294.4 98.5 %collective-permute-start.52 = (bf16[2,2,384,384]{3,2,1,0:T(8,128)(2,1)}, bf16[2,2,384,384]{3,2,1,0:T(8,128)(2,1)S(1)}, u32[]{:S(2)}, u32[]{:S(2)}) collective-permute-start(bf16[2,2,384,384]{3,2,1,0:T(8,128)(2,1)} %pad_maximum_fusion.14), channel_id=1, source_target_pairs={{0,2},{1,3},{2,0},{3,1},{4,6},{5,7},{6,4},{7,5},{8,10},{9,11},{10,... | collective-permute-start | bytes 3538952 | tf_op jit(solution)/shard_map/ppermute | solution.py:38
  297.4 96.7 %collective-permute-start.50 = (bf16[2,2,384,384]{3,2,1,0:T(8,128)(2,1)}, bf16[2,2,384,384]{3,2,1,0:T(8,128)(2,1)}, u32[]{:S(2)}, u32[]{:S(2)}) collective-permute-start(bf16[2,2,384,384]{3,2,1,0:T(8,128)(2,1)} %pad_maximum_fusion.13), channel_id=1, source_target_pairs={{0,1},{1,0},{2,3},{3,2},{4,5},{5,4},{6,7},{7,6},{8,9},{9,8},{10,11... | collective-permute-start | bytes 3538952 | tf_op jit(solution)/shard_map/ppermute | solution.py:38
  306.5 90.5 %collective-permute-start.44 = (bf16[4,96,768]{2,1,0:T(8,128)(2,1)S(1)}, bf16[4,96,768]{2,1,0:T(8,128)(2,1)}, u32[]{:S(2)}, u32[]{:S(2)}) collective-permute-start(bf16[4,96,768]{2,1,0:T(8,128)(2,1)S(1)} %dynamic-slice_convert_fusion), channel_id=1, source_target_pairs={{0,4},{4,0},{1,5},{5,1},{2,6},{6,2},{3,7},{7,3},{8,12},{12,8},{9,1... | collective-permute-start | bytes 1769480 | tf_op jit(solution)/shard_map/ppermute | solution.py:38
  392.5 32.1 %collective-permute-start.40 = (bf16[288,768]{1,0:T(8,128)(2,1)}, bf16[288,768]{1,0:T(8,128)(2,1)}, u32[]{:S(2)}, u32[]{:S(2)}) collective-permute-start(bf16[288,768]{1,0:T(8,128)(2,1)} %collective-permute-done.36), channel_id=1, source_target_pairs={{0,2},{1,3},{2,0},{3,1},{4,6},{5,7},{6,4},{7,5},{8,10},{9,11},{10,... | collective-permute-start | bytes 1327112 | tf_op jit(solution)/shard_map/ppermute | solution.py:38
  392.9 31.8 %collective-permute-start.41 = (bf16[288,768]{1,0:T(8,128)(2,1)}, bf16[288,768]{1,0:T(8,128)(2,1)}, u32[]{:S(2)}, u32[]{:S(2)}) collective-permute-start(bf16[288,768]{1,0:T(8,128)(2,1)} %collective-permute-done.39), channel_id=1, source_target_pairs={{0,1},{1,0},{2,3},{3,2},{4,5},{5,4},{6,7},{7,6},{8,9},{9,8},{10,11... | collective-permute-start | bytes 1327112 | tf_op jit(solution)/shard_map/ppermute | solution.py:38
  418.1 50.8 %reduce-scatter.10.cloned.1.call-start = ((), (), s32[]{:S(2)}) async-start(), calls=%async_computation.4 | async-start | bytes 737280
  423.1 77.6 %reduce-scatter.8.cloned.1.call-start = ((), (), s32[]{:S(2)}) async-start(), calls=%async_computation.3 | async-start | bytes 1474560 | tf_op jit(solution)/shard_map/reduce_scatter | solution.py:603
  469.8 32.8 %collective-permute-start.43 = (bf16[192,288]{0,1:T(8,128)(2,1)S(1)}, bf16[192,288]{0,1:T(8,128)(2,1)S(1)}, u32[]{:S(2)}, u32[]{:S(2)}) collective-permute-start(bf16[192,288]{0,1:T(8,128)(2,1)S(1)} %bitcast.267), channel_id=1, source_target_pairs={{0,4},{4,0},{1,5},{5,1},{2,6},{6,2},{3,7},{7,3},{8,12},{12,8},{9,1... | collective-permute-start | bytes 331784 | tf_op jit(solution)/shard_map/ppermute | solution.py:38
  (78 other events, 898.1 us)
Sparse Core Ops, SparseCore 0:
  418.2 27.3 reduce-scatter.11
  448.5 20.2 reduce-scatter.9
  471.3 29.4 reduce-scatter.7
